TPU v7x, 256 devices: a whole 4x4x8 slice. The times are simulated.
256 devices in a mesh: seq: 32 (over x, z), head: 8 (over y, core).
Axes of the slice: x: 4, y: 4, z: 8, core: 2. Of those that a mesh axis runs over, the one named last changes fastest.
Arguments:
- queries: bfloat16 [4, 256, 64, 128], P(None, 'seq', 'head')
- new_kv: bfloat16 [2, 4, 256, 8, 128], P(None, None, 'seq', 'head'), may hold values from -12 to 12
- prompt_keys: bfloat16 [8, 32768, 8, 128], P(None, 'seq', 'head')
- prompt_values: bfloat16 [8, 32768, 8, 128], P(None, 'seq', 'head'), may hold values from -6 to 6
- suffix_kv: bfloat16 [2, 256, 512, 8, 128], P(None, 'seq', None, 'head'), may hold values from -9.5625 to 9.5625
- prompt_ids: int32 [256, 1], P('seq'), may hold values from 0 to 7
- suffix_lengths: int32 [256], P('seq'), may hold values from 1 to 512, 65536 in all
- token_ids: int32 [256, 4], replicated, may hold values from 0 to 65535
- embedding: bfloat16 [65536, 8192], P('head', 'seq'), may hold values from -3 to 3
- out_weight: bfloat16 [8192, 8192], P('head', 'seq'), may hold values from -0.25 to 0.25
Outputs:
- hidden_out: bfloat16 [256, 4, 8192], P('head', None, 'seq')
Inputs may be any that keep to these rules, and one draw needn't show every extreme that they name: `prompt_ids`: every one of the 8 prompts is named by some row.
All inputs are finite; a program needn't handle non-finite values. No bound on the sum of `suffix_lengths` on one device may be relied on, other than what follows from the above.
Results may differ from a plain program's by a relative error of at most 0.02.
Values may be sent and summed in bfloat16 or wider, within the bound.
No kernel may reach another device: no remote copies, remote signals or barrier semaphores. Data moves between devices by JAX's collectives and lax.ppermute only.
A program may use at most 320 MiB of HBM per device.

v0:
```python
import math

import jax
import jax.numpy as jnp
from jax import lax
from jax.sharding import PartitionSpec as P


def shards(
    queries,
    new_kv,
    prompt_keys,
    prompt_values,
    suffix_kv,
    prompt_ids,
    suffix_lengths,
    token_ids,
    embedding,
    out_weight,
):
    step_count, rows_own, heads_own, head_dim = queries.shape
    kv_own = prompt_keys.shape[2]
    group_size = heads_own // kv_own
    score_scale = head_dim ** (-0.5)
    prompt_total = prompt_keys.shape[0]
    gathered_q, gathered_ids = (
        lax.all_gather(queries, "seq", axis=1, tiled=True),
        lax.all_gather(prompt_ids.reshape(1, rows_own), "seq", axis=1, tiled=True),
    )
    all_rows = gathered_q.shape[1]
    block_rows = math.gcd(all_rows, 32)
    row_ids = gathered_ids[0].astype(jnp.int32)
    order = jnp.argsort(row_ids, stable=True)
    inverse = jnp.argsort(order, stable=True)
    counts = jnp.sum(
        (row_ids[:, None] == jnp.arange(prompt_total, dtype=jnp.int32)[None, :]).astype(jnp.int32),
        axis=0,
    )
    starts = jnp.cumsum(counts) - counts
    sorted_q = jnp.take(gathered_q, order, axis=1)
    padding = jnp.zeros((step_count, block_rows, heads_own, head_dim), sorted_q.dtype)
    sorted_q = jnp.concatenate([sorted_q, padding], axis=1).reshape(
        step_count, all_rows + block_rows, kv_own, group_size, head_dim
    )
    padded_rows = all_rows + block_rows
    init_peak = jnp.zeros((padded_rows, kv_own, step_count, group_size), jnp.float32)
    init_mixed = jnp.zeros((padded_rows, kv_own, step_count, group_size, head_dim), jnp.float32)

    def per_prompt(prompt_index, carry):
        key_rows = lax.dynamic_index_in_dim(prompt_keys, prompt_index, 0, keepdims=False)
        value_rows = lax.dynamic_index_in_dim(prompt_values, prompt_index, 0, keepdims=False)
        first = starts[prompt_index]
        limit = first + counts[prompt_index]
        tiles = (counts[prompt_index] + block_rows - 1) // block_rows

        def per_tile(tile_index, inner):
            peak_acc, total_acc, mixed_acc = inner
            begin = first + tile_index * block_rows
            query_block = lax.dynamic_slice_in_dim(sorted_q, begin, block_rows, 1)
            scores = (
                jnp.einsum(
                    "trcgd,kcd->rctgk", query_block, key_rows, preferred_element_type=jnp.float32
                )
                * score_scale
            )
            peak = jnp.max(scores, axis=-1)
            weights = jnp.exp(scores - peak[..., None])
            total = jnp.sum(weights, axis=-1)
            mixed = jnp.einsum(
                "rctgk,kcd->rctgd",
                weights.astype(jnp.bfloat16),
                value_rows,
                preferred_element_type=jnp.float32,
            )
            valid = begin + jnp.arange(block_rows, dtype=jnp.int32) < limit
            old_peak = lax.dynamic_slice_in_dim(peak_acc, begin, block_rows, 0)
            old_total = lax.dynamic_slice_in_dim(total_acc, begin, block_rows, 0)
            old_mixed = lax.dynamic_slice_in_dim(mixed_acc, begin, block_rows, 0)
            flag = valid[:, None, None, None]
            peak_acc = lax.dynamic_update_slice_in_dim(
                peak_acc, jnp.where(flag, peak, old_peak), begin, 0
            )
            total_acc = lax.dynamic_update_slice_in_dim(
                total_acc, jnp.where(flag, total, old_total), begin, 0
            )
            mixed_acc = lax.dynamic_update_slice_in_dim(
                mixed_acc, jnp.where(flag[..., None], mixed, old_mixed), begin, 0
            )
            return (peak_acc, total_acc, mixed_acc)

        return lax.fori_loop(0, tiles, per_tile, carry)

    peak_sorted, total_sorted, mixed_sorted = lax.fori_loop(
        0, prompt_total, per_prompt, (init_peak, init_peak, init_mixed)
    )
    highest = jnp.take(peak_sorted[:all_rows], inverse, axis=0)
    summed = jnp.take(total_sorted[:all_rows], inverse, axis=0)
    blended = jnp.take(mixed_sorted[:all_rows], inverse, axis=0)
    first_row = lax.axis_index("seq") * rows_own
    global_peak = lax.pmax(highest.astype(jnp.bfloat16), "seq").astype(highest.dtype)
    factor = jnp.exp(highest - global_peak)
    own_total, own_mixed = (
        lax.psum_scatter(
            (summed * factor).astype(jnp.bfloat16), "seq", scatter_dimension=0, tiled=True
        ).astype(jnp.float32),
        lax.psum_scatter(
            (blended * factor[..., None]).astype(jnp.bfloat16),
            "seq",
            scatter_dimension=0,
            tiled=True,
        ).astype(jnp.float32),
    )
    own_peak = lax.dynamic_slice_in_dim(global_peak, first_row, rows_own, 0)
    own_q = queries.reshape(step_count, rows_own, kv_own, group_size, head_dim)
    suffix_len = suffix_kv.shape[2]
    score_suffix = (
        jnp.einsum("trcgd,rkcd->rctgk", own_q, suffix_kv[0], preferred_element_type=jnp.float32)
        * score_scale
    )
    live_mask = jnp.arange(suffix_len, dtype=jnp.int32)[None, :] < suffix_lengths[:, None]
    score_suffix = jnp.where(live_mask[:, None, None, None, :], score_suffix, -jnp.inf)
    score_fresh = (
        jnp.einsum("trcgd,urcd->rctgu", own_q, new_kv[0], preferred_element_type=jnp.float32)
        * score_scale
    )
    step_order = jnp.arange(step_count, dtype=jnp.int32)
    causal = step_order[None, :] <= step_order[:, None]
    score_fresh = jnp.where(causal[None, None, :, None, :], score_fresh, -jnp.inf)
    peak_all = jnp.maximum(
        own_peak, jnp.maximum(jnp.max(score_suffix, axis=-1), jnp.max(score_fresh, axis=-1))
    )
    carried = jnp.exp(own_peak - peak_all)
    weight_suffix = jnp.exp(score_suffix - peak_all[..., None])
    weight_fresh = jnp.exp(score_fresh - peak_all[..., None])
    denominator = (
        own_total * carried + jnp.sum(weight_suffix, axis=-1) + jnp.sum(weight_fresh, axis=-1)
    )
    numerator = own_mixed * carried[..., None]
    numerator = numerator + jnp.einsum(
        "rctgk,rkcd->rctgd",
        weight_suffix.astype(jnp.bfloat16),
        suffix_kv[1],
        preferred_element_type=jnp.float32,
    )
    numerator = numerator + jnp.einsum(
        "rctgu,urcd->rctgd",
        weight_fresh.astype(jnp.bfloat16),
        new_kv[1],
        preferred_element_type=jnp.float32,
    )
    attention = (numerator / denominator[..., None]).astype(jnp.bfloat16)
    attention_all = lax.all_gather(attention, "seq", axis=0, tiled=True)
    weight_local = out_weight.reshape(kv_own, group_size, head_dim, out_weight.shape[1])
    vocab_own = embedding.shape[0]
    vocab_first = lax.axis_index("head") * vocab_own
    projected = jnp.einsum(
        "rctgd,cgde->rte", attention_all, weight_local, preferred_element_type=jnp.float32
    )
    local_ids = token_ids - vocab_first
    inside = (local_ids >= 0) & (local_ids < vocab_own)
    embedded = jnp.take(embedding, jnp.clip(local_ids, 0, vocab_own - 1), axis=0).astype(
        jnp.float32
    )
    return lax.psum_scatter(
        (projected + jnp.where(inside[..., None], embedded, 0.0)).astype(jnp.bfloat16),
        "head",
        scatter_dimension=0,
        tiled=True,
    )


def solution(mesh):
    return jax.shard_map(
        shards,
        mesh=mesh,
        in_specs=(
            P(None, "seq", "head", None),
            P(None, None, "seq", "head", None),
            P(None, "seq", "head", None),
            P(None, "seq", "head", None),
            P(None, "seq", None, "head", None),
            P("seq", None),
            P("seq"),
            P(),
            P("head", "seq"),
            P("head", "seq"),
        ),
        out_specs=P("head", None, "seq"),
        check_vma=False,
    )
```

profile of v0, /device:TPU:1, one launch (start us, length us, event | category | flops | bytes accessed | tf_op | source)
XLA Modules:
  0.0 740.5 jit_solution(6251712479876725791)
XLA Ops:
  10.1 20.0 %all-reduce.1 = s32[256]{0:T(256)S(1)} all-reduce(s32[256]{0:T(256)S(1)} %bitcast_dynamic-update-slice_fusion), channel_id=2, replica_groups=mesh['seq'=32,'head'=8] {'seq'}, use_global_device_ids=true, to_apply=%add.1 | all-reduce | flops 256 | bytes 2048 | tf_op jit(solution)/shard_map/squeeze | solution.py:32
  30.5 3.2 sort.31
  33.6 3.2 sort.32
  36.9 51.5 %all-gather.4.cloned.1.call-done = bf16[4,256,8,128]{3,2,1,0:T(8,128)(2,1)} async-done(((bf16[4,8,8,128]{3,2,1,0:T(8,128)(2,1)}), bf16[4,256,8,128]{3,2,1,0:T(8,128)(2,1)}) %all-gather.4.cloned.1.call-update) | async-done | bytes 2097168 | tf_op jit(solution)/shard_map/all_gather | solution.py:27
  88.4 2.9 gather_fusion
  92.7 1.9 copy.55
  96.3 2.7 broadcast_in_dim.125
  99.0 145.6 %while.65 = (s32[]{:T(128)}, f32[288,1,4,8]{3,0,2,1:T(8,128)}, f32[288,1,4,8]{3,0,2,1:T(8,128)}, f32[288,1,4,8,128]{4,3,2,0,1:T(8,128)}, s32[8]{0:T(128)S(1)}, /...) while((s32[]{:T(128)}, f32[288,1,4,8]{3,0,2,1:T(8,128)}, ...), condition=%wide.region_9.10_spmd, body=%wide.region_4.9_spmd.sunk | while | flops 543293504 | bytes 15520562 | solution.py:93
  103.4 20.1 %while.66 = (s32[]{:T(128)}, f32[288,1,4,8]{3,0,2,1:T(8,128)}, f32[288,1,4,8]{3,0,2,1:T(8,128)}, f32[288,1,4,8,128]{4,3,2,0,1:T(8,128)}, s32[]{:T(128)}, /*index...) while((s32[]{:T(128)}, f32[288,1,4,8]{3,0,2,1:T(8,128)}, ...), condition=%wide.region_8.8_spmd, body=%wide.region_5.7_spmd.sunk | while | flops 543293504 | bytes 14471491 | solution.py:91
  104.1 1.7 bitcast_reduce_fusion.2
  107.8 1.6 dynamic_update_slice.14
  110.9 2.5 fusion.70
  114.1 1.8 bitcast_reduce_fusion.2
  117.8 1.6 dynamic_update_slice.14
  119.4 1.5 dynamic_update_slice.15
  120.9 2.6 fusion.70
  127.9 10.1 %while.66 = (s32[]{:T(128)}, f32[288,1,4,8]{3,0,2,1:T(8,128)}, f32[288,1,4,8]{3,0,2,1:T(8,128)}, f32[288,1,4,8,128]{4,3,2,0,1:T(8,128)}, s32[]{:T(128)}, /*index...) while((s32[]{:T(128)}, f32[288,1,4,8]{3,0,2,1:T(8,128)}, ...), condition=%wide.region_8.8_spmd, body=%wide.region_5.7_spmd.sunk | while | flops 543293504 | bytes 14471491 | solution.py:91
  128.5 1.7 bitcast_reduce_fusion.2
  132.3 1.6 dynamic_update_slice.14
  133.8 1.6 dynamic_update_slice.15
  135.4 2.5 fusion.70
  142.3 10.1 %while.66 = (s32[]{:T(128)}, f32[288,1,4,8]{3,0,2,1:T(8,128)}, f32[288,1,4,8]{3,0,2,1:T(8,128)}, f32[288,1,4,8,128]{4,3,2,0,1:T(8,128)}, s32[]{:T(128)}, /*index...) while((s32[]{:T(128)}, f32[288,1,4,8]{3,0,2,1:T(8,128)}, ...), condition=%wide.region_8.8_spmd, body=%wide.region_5.7_spmd.sunk | while | flops 543293504 | bytes 14471491 | solution.py:91
  143.0 1.7 bitcast_reduce_fusion.2
  146.7 1.6 dynamic_update_slice.14
  148.3 1.6 dynamic_update_slice.15
  149.8 2.6 fusion.70
  156.8 10.1 %while.66 = (s32[]{:T(128)}, f32[288,1,4,8]{3,0,2,1:T(8,128)}, f32[288,1,4,8]{3,0,2,1:T(8,128)}, f32[288,1,4,8,128]{4,3,2,0,1:T(8,128)}, s32[]{:T(128)}, /*index...) while((s32[]{:T(128)}, f32[288,1,4,8]{3,0,2,1:T(8,128)}, ...), condition=%wide.region_8.8_spmd, body=%wide.region_5.7_spmd.sunk | while | flops 543293504 | bytes 14471491 | solution.py:91
  157.5 1.8 bitcast_reduce_fusion.2
  161.2 1.6 dynamic_update_slice.14
  164.3 2.6 fusion.70
  171.3 10.0 %while.66 = (s32[]{:T(128)}, f32[288,1,4,8]{3,0,2,1:T(8,128)}, f32[288,1,4,8]{3,0,2,1:T(8,128)}, f32[288,1,4,8,128]{4,3,2,0,1:T(8,128)}, s32[]{:T(128)}, /*index...) while((s32[]{:T(128)}, f32[288,1,4,8]{3,0,2,1:T(8,128)}, ...), condition=%wide.region_8.8_spmd, body=%wide.region_5.7_spmd.sunk | while | flops 543293504 | bytes 14471491 | solution.py:91
  171.9 1.8 bitcast_reduce_fusion.2
  175.7 1.6 dynamic_update_slice.14
  178.8 2.5 fusion.70
  185.7 10.1 %while.66 = (s32[]{:T(128)}, f32[288,1,4,8]{3,0,2,1:T(8,128)}, f32[288,1,4,8]{3,0,2,1:T(8,128)}, f32[288,1,4,8,128]{4,3,2,0,1:T(8,128)}, s32[]{:T(128)}, /*index...) while((s32[]{:T(128)}, f32[288,1,4,8]{3,0,2,1:T(8,128)}, ...), condition=%wide.region_8.8_spmd, body=%wide.region_5.7_spmd.sunk | while | flops 543293504 | bytes 14471491 | solution.py:91
  186.4 1.8 bitcast_reduce_fusion.2
  190.1 1.6 dynamic_update_slice.14
  193.2 2.6 fusion.70
  200.2 20.1 %while.66 = (s32[]{:T(128)}, f32[288,1,4,8]{3,0,2,1:T(8,128)}, f32[288,1,4,8]{3,0,2,1:T(8,128)}, f32[288,1,4,8,128]{4,3,2,0,1:T(8,128)}, s32[]{:T(128)}, /*index...) while((s32[]{:T(128)}, f32[288,1,4,8]{3,0,2,1:T(8,128)}, ...), condition=%wide.region_8.8_spmd, body=%wide.region_5.7_spmd.sunk | while | flops 543293504 | bytes 14471491 | solution.py:91
  200.8 1.8 bitcast_reduce_fusion.2
  204.5 1.6 dynamic_update_slice.14
  207.7 2.6 fusion.70
  210.9 1.8 bitcast_reduce_fusion.2
  214.6 1.6 dynamic_update_slice.14
  217.7 2.6 fusion.70
  224.6 20.0 %while.66 = (s32[]{:T(128)}, f32[288,1,4,8]{3,0,2,1:T(8,128)}, f32[288,1,4,8]{3,0,2,1:T(8,128)}, f32[288,1,4,8,128]{4,3,2,0,1:T(8,128)}, s32[]{:T(128)}, /*index...) while((s32[]{:T(128)}, f32[288,1,4,8]{3,0,2,1:T(8,128)}, ...), condition=%wide.region_8.8_spmd, body=%wide.region_5.7_spmd.sunk | while | flops 543293504 | bytes 14471491 | solution.py:91
  225.3 1.7 bitcast_reduce_fusion.2
  229.0 1.6 dynamic_update_slice.14
  232.1 2.6 fusion.70
  235.3 1.8 bitcast_reduce_fusion.2
  239.0 1.5 dynamic_update_slice.14
  242.1 2.5 fusion.70
  247.4 114.8 %pmax.7 = bf16[256,1,4,8]{3,2,0,1:T(4,128)(2,1)S(1)} all-reduce(bf16[256,1,4,8]{3,2,0,1:T(4,128)(2,1)S(1)} %fusion.46), channel_id=1, replica_groups=mesh['seq'=32,'head'=8] {'seq'}, use_global_device_ids=true, to_apply=%region_10.12 | all-reduce | flops 8192 | bytes 32768 | tf_op jit(solution)/shard_map/pmax | solution.py:100
  362.3 4.6 slice_bitcast_fusion
  366.9 5.0 gather_fusion.1
  374.4 5.5 fusion.22
  381.1 1.8 fusion.60
  382.9 112.3 %all-reduce.2 = bf16[256,1,4,8]{3,2,0,1:T(4,128)(2,1)S(1)} all-reduce(bf16[256,1,4,8]{3,2,0,1:T(4,128)(2,1)S(1)} %get-tuple-element.487), channel_id=4, replica_groups=mesh['seq'=32,'head'=8] {'seq'}, use_global_device_ids=true, to_apply=%region_14.16.clone | all-reduce | flops 8192 | bytes 32768
  495.9 120.5 %reduce-scatter.4.cloned.1.call-done = bf16[8,1,4,8,128]{4,3,2,0,1:T(8,128)(2,1)} async-done(((bf16[256,1,4,8,128]{4,3,2,0,1:T(8,128)(2,1)}), bf16[8,1,4,8,128]{4,3,2,0,1:T(8,128)(2,1)}) %reduce-scatter.4.cloned.1.call-update) | async-done | bytes 65552 | tf_op jit(solution)/shard_map/reduce_scatter | solution.py:106
  616.4 2.2 fusion.40
  619.0 6.2 gather_fusion.2
  625.3 71.4 %all-gather.6.cloned.1.call-done = bf16[256,1,4,8,128]{4,3,2,1,0:T(8,128)(2,1)} async-done(((bf16[8,1,4,8,128]{4,3,2,1,0:T(8,128)(2,1)}), bf16[256,1,4,8,128]{4,3,2,1,0:T(8,128)(2,1)}) %all-gather.6.cloned.1.call-update) | async-done | bytes 2097168 | tf_op jit(solution)/shard_map/all_gather | solution.py:152
  696.7 3.3 fusion.32
  700.0 32.4 %reduce-scatter.6.cloned.1.call-done = bf16[32,4,256]{2,0,1:T(8,128)(2,1)} async-done(((bf16[256,4,256]{2,0,1:T(8,128)(2,1)}), bf16[32,4,256]{2,0,1:T(8,128)(2,1)}) %reduce-scatter.6.cloned.1.call-update) | async-done | bytes 65552 | tf_op jit(solution)/shard_map/reduce_scatter | solution.py:164
  (127 shorter events, 67.5 us)
Async XLA Ops:
  6.5 690.1 %copy-start = (bf16[1024,256]{1,0:T(8,128)(2,1)S(1)}, bf16[1024,256]{1,0:T(8,128)(2,1)}, u32[]{:S(2)}) copy-start(bf16[1024,256]{1,0:T(8,128)(2,1)} %param.25) | copy-start | bytes 1572868
  6.5 81.9 %all-gather.4.cloned.1.call-start = ((), (), s32[]{:S(2)}) async-start(), calls=%async_computation.2 | async-start | bytes 2162688 | tf_op jit(solution)/shard_map/all_gather | solution.py:27
  7.3 609.1 %reduce-scatter.4.cloned.1.call-start = ((), (), s32[]{:S(2)}) async-start(), calls=%async_computation.3 | async-start | bytes 2162688 | tf_op jit(solution)/shard_map/reduce_scatter | solution.py:106
  366.9 5.0 copy-start.1
  374.3 6.2 copy-start.5
  374.3 6.3 copy-start.3
  374.4 6.3 copy-start.2
  379.9 316.8 %all-gather.6.cloned.1.call-start = ((), (), s32[]{:S(2)}) async-start(), calls=%async_computation.4 | async-start | bytes 2162688 | tf_op jit(solution)/shard_map/all_gather | solution.py:152
  382.8 235.8 %copy-start.4 = (s32[256,4]{0,1:T(4,128)S(1)}, s32[256,4]{0,1:T(4,128)}, u32[]{:S(2)}) copy-start(s32[256,4]{0,1:T(4,128)} %param.23) | copy-start | bytes 12292
  618.6 113.8 %reduce-scatter.6.cloned.1.call-start = ((), (), s32[]{:S(2)}) async-start(), calls=%async_computation.5 | async-start | bytes 589824 | tf_op jit(solution)/shard_map/reduce_scatter | solution.py:164
Sparse Core Ops, SparseCore 0:
  9.9 78.3 all-gather.3
  380.0 236.3 reduce-scatter.3
  619.3 77.2 all-gather.5
  700.1 32.2 reduce-scatter.5
where the time goes:
time: 745 us; the launch traced here: 740 us
  waiting for transfers between devices  277 us (37%)
  blocking collectives  247 us (33%)
  local copies, waits for them, and re-layouts  86.3 us (12%)
  matrix products  55.2 us (7%)
  other arithmetic  36.6 us (5%)
  loops' own time  23.7 us (3%)
  between operations  14.7 us (2%)
    reduce_scatter x1, waiting for transfers between devices, shards(): lax.psum_scatter((blended * factor[..., None]).astype(jnp.bfloat16), 'seq...  121 us
    pmax x1, blocking collectives, shards(): lax.pmax(highest.astype(jnp.bfloat16), 'seq').astype(highest.dtype)  115 us
    unnamed x1, blocking collectives  112 us
    all_gather x1, waiting for transfers between devices, shards(): attention_all = lax.all_gather(attention, 'seq', axis=0, tiled=True)  71.4 us
    all_gather x1, waiting for transfers between devices, shards(): lax.all_gather(queries, 'seq', axis=1, tiled=True)  51.5 us
    reduce_scatter x1, waiting for transfers between devices, shards(): lax.psum_scatter((projected + jnp.where(inside[..., None], embedded, 0.0)...  32.4 us
    dot_general x11, matrix products, per_tile(): jnp.einsum('rctgk,kcd->rctgd', weights.astype(jnp.bfloat16), value_rows,...  28.1 us
    squeeze x1, blocking collectives, shards(): row_ids = gathered_ids[0].astype(jnp.int32)  20 us
  transfers between devices with their start and end apart: 4, of which 4 were waited for; matrix products, arithmetic and copies ran while one was open for 2% of the time, Pallas kernels for 0%

commit v1 on v0

v1 whole, which is shorter than its diff:
```python
import functools
import math

import jax
import jax.numpy as jnp
from jax import lax
from jax.experimental import pallas as pl
from jax.experimental.pallas import tpu as pltpu
from jax.sharding import PartitionSpec as P

BLOCK_ROWS = 8
PACK = 16
LOG2E = 1.0 / math.log(2.0)
SEQ_X, SEQ_Z = 4, 8
Z_GROUPS = [[x * SEQ_Z + z for z in range(SEQ_Z)] for x in range(SEQ_X)]
X_GROUPS = [[x * SEQ_Z + z for x in range(SEQ_X)] for z in range(SEQ_Z)]
VMEM = pl.BlockSpec(memory_space=pltpu.VMEM)
SMEM = pl.BlockSpec(memory_space=pltpu.SMEM)


def three_terms(x):
    hi = x.astype(jnp.bfloat16).astype(jnp.float32)
    mid = (x - hi).astype(jnp.bfloat16).astype(jnp.float32)
    return hi, mid, (x - hi) - mid


def prompt_kernel(per_row, scale, slot_ref, count_ref, q_ref, k_ref, v_ref, out_ref, stat_ref):
    owners = out_ref.shape[0]
    queries = BLOCK_ROWS * per_row
    body_rows = BLOCK_ROWS * per_row

    def block(b, carry):
        rows = []
        for j in range(BLOCK_ROWS):
            rows.append(slot_ref[b * BLOCK_ROWS + j] // 8)
        prompt = slot_ref[b * BLOCK_ROWS] % 8
        where = [(r // 8, pl.ds(pl.multiple_of((r % 8) * per_row, per_row), per_row)) for r in rows]
        q = jnp.concatenate([q_ref[o, w, :] for o, w in where], axis=0)
        s = lax.dot_general(
            q, k_ref[prompt], (((1,), (1,)), ((), ())), preferred_element_type=jnp.float32
        )
        top = jnp.max(s, axis=-1, keepdims=True) * scale
        p = jnp.exp2(s * scale - top)
        total = jnp.sum(p, axis=-1, keepdims=True)
        mixed = jnp.dot(
            p.astype(jnp.bfloat16), v_ref[prompt], preferred_element_type=jnp.float32
        )
        mixed = (mixed / total).astype(jnp.bfloat16)
        hi, mid, lo = three_terms(top)
        lane = lax.broadcasted_iota(jnp.int32, (queries, 128), 1)
        at = lax.broadcasted_iota(jnp.int32, (queries, 128), 0) % per_row
        part = lane // per_row
        stat = jnp.where(part == 0, hi, jnp.where(part == 1, mid, jnp.where(part == 2, lo, total)))
        stat = jnp.where(lane % per_row == at, stat, 0.0)
        stat = jnp.sum(stat.reshape(BLOCK_ROWS, per_row, 128), axis=1)
        for j in range(BLOCK_ROWS):
            o, w = where[j]
            out_ref[o, w, :] = mixed[j * per_row : (j + 1) * per_row, :]
            stat_ref[pl.ds(rows[j], 1), :] = stat[j : j + 1, :]
        return carry

    lax.fori_loop(0, count_ref[0], block, 0)
    for o in range(owners):
        stats = jnp.concatenate(
            [stat_ref[o * 8 : (o + 1) * 8, :], jnp.zeros((PACK - 8, 128), jnp.float32)], axis=0
        )
        out_ref[o, body_rows : body_rows + PACK, :] = stats.astype(jnp.bfloat16)


def own_kernel(per_row, steps, scale, len_ref, q_ref, kv_ref, fresh_ref, out_ref, top_ref, total_ref):
    rows, length = kv_ref.shape[1], kv_ref.shape[2]
    group = per_row // steps
    pos = lax.broadcasted_iota(jnp.int32, (per_row, length), 1)
    step_of = lax.broadcasted_iota(jnp.int32, (per_row, PACK), 0) // group
    fresh_at = lax.broadcasted_iota(jnp.int32, (per_row, PACK), 1)
    over_last = (((1,), (1,)), ((), ()))
    for j in range(rows):
        part = pl.ds(j * per_row, per_row)
        q = q_ref[part, :]
        s = lax.dot_general(q, kv_ref[0, j], over_last, preferred_element_type=jnp.float32)
        s = jnp.where(pos < len_ref[j], s * scale, -jnp.inf)
        f = lax.dot_general(q, fresh_ref[0, j], over_last, preferred_element_type=jnp.float32)
        f = jnp.where(fresh_at <= step_of, f * scale, -jnp.inf)
        top = jnp.maximum(
            jnp.max(s, axis=-1, keepdims=True), jnp.max(f, axis=-1, keepdims=True)
        )
        ps, pf = jnp.exp2(s - top), jnp.exp2(f - top)
        total = jnp.sum(ps, axis=-1, keepdims=True) + jnp.sum(pf, axis=-1, keepdims=True)
        mixed = jnp.dot(ps.astype(jnp.bfloat16), kv_ref[1, j], preferred_element_type=jnp.float32)
        mixed += jnp.dot(
            pf.astype(jnp.bfloat16), fresh_ref[1, j], preferred_element_type=jnp.float32
        )
        out_ref[part, :] = mixed
        top_ref[part, :] = jnp.broadcast_to(top, (per_row, 128))
        total_ref[part, :] = jnp.broadcast_to(total, (per_row, 128))


def merge_kernel(per_row, parts_ref, own_ref, top_ref, total_ref, out_ref):
    sources = parts_ref.shape[0]
    rows = 8
    stat = parts_ref[:, rows * per_row : rows * per_row + PACK, :].astype(jnp.float32)[:, :rows, :]
    stat = stat.reshape(sources * rows, 128)
    top = (
        stat
        + pltpu.roll(stat, 128 - per_row, 1)
        + pltpu.roll(stat, 128 - 2 * per_row, 1)
    )
    total = pltpu.roll(stat, 128 - 3 * per_row, 1)
    top = top.reshape(sources, rows, 128)
    total = total.reshape(sources, rows, 128)
    peak = jnp.max(top, axis=0)
    weight = total * jnp.exp2(top - peak[None])
    summed = jnp.sum(weight, axis=0)
    for j in range(rows):
        table = jnp.concatenate(
            [weight[:, j, :], peak[j : j + 1, :], summed[j : j + 1, :], jnp.zeros((6, 128), jnp.float32)],
            axis=0,
        )
        table = jnp.transpose(table)[:per_row, :]
        span = slice(j * per_row, (j + 1) * per_row)
        acc = jnp.zeros((per_row, 128), jnp.float32)
        for i in range(sources):
            acc += table[:, i : i + 1] * parts_ref[i, span, :].astype(jnp.float32)
        prompt_top = table[:, sources : sources + 1]
        prompt_sum = table[:, sources + 1 : sources + 2]
        own_top = top_ref[span, :]
        best = jnp.maximum(prompt_top, own_top)
        a, b = jnp.exp2(prompt_top - best), jnp.exp2(own_top - best)
        num = acc * a + own_ref[span, :] * b
        den = prompt_sum * a + total_ref[span, :] * b
        out_ref[span, :] = (num / den).astype(jnp.bfloat16)


def slots(ids, prompts):
    rows = ids.shape[0]
    blocks = rows // BLOCK_ROWS + prompts
    r = jnp.arange(rows, dtype=jnp.int32)
    p = jnp.arange(prompts, dtype=jnp.int32)
    named = ids[None, :] == p[:, None]
    need = (jnp.sum(named.astype(jnp.int32), axis=1) + BLOCK_ROWS - 1) // BLOCK_ROWS
    first = jnp.sum(jnp.where(p[None, :] < p[:, None], need[None, :], 0), axis=1) * BLOCK_ROWS
    before = jnp.sum(
        ((ids[None, :] == ids[:, None]) & (r[None, :] < r[:, None])).astype(jnp.int32), axis=1
    )
    place = jnp.sum(jnp.where(named, first[:, None], 0), axis=0) + before
    code = (place * rows + r) * 8 + ids
    k = jnp.arange(blocks * BLOCK_ROWS, dtype=jnp.int32)
    best = jnp.max(jnp.where(place[None, :] <= k[:, None], code[None, :], 0), axis=1)
    return best % (rows * 8), jnp.sum(need).reshape(1)


def spread(x, groups):
    n = len(groups[0])
    return lax.all_to_all(
        jnp.broadcast_to(x[None], (n,) + x.shape), "seq", 0, 0, axis_index_groups=groups
    )


def gather_seq(x):
    zs = spread(x, Z_GROUPS)
    xs = spread(zs, X_GROUPS)
    return xs.reshape((SEQ_X * SEQ_Z,) + x.shape)


def shards(
    queries,
    new_kv,
    prompt_keys,
    prompt_values,
    suffix_kv,
    prompt_ids,
    suffix_lengths,
    token_ids,
    embedding,
    out_weight,
):
    steps, rows_own, heads_own, head_dim = queries.shape
    prompts, positions = prompt_keys.shape[0], prompt_keys.shape[1]
    per_row = steps * heads_own
    scale = head_dim ** (-0.5) * LOG2E
    own_q = jnp.transpose(queries, (1, 0, 2, 3)).reshape(rows_own * per_row, head_dim)
    id_rows = jnp.broadcast_to(prompt_ids.astype(jnp.bfloat16), (rows_own, head_dim))
    packed = jnp.concatenate([own_q, id_rows, jnp.zeros((PACK - rows_own, head_dim), jnp.bfloat16)])
    all_q = gather_seq(packed)
    sources = all_q.shape[0]
    ids = all_q[:, rows_own * per_row : rows_own * per_row + rows_own, 0].reshape(-1)
    slot, count = slots(ids.astype(jnp.int32), prompts)

    payload = jax.ShapeDtypeStruct((sources, rows_own * per_row + PACK, head_dim), jnp.bfloat16)
    partial = pl.pallas_call(
        functools.partial(prompt_kernel, per_row, scale),
        out_shape=payload,
        in_specs=[SMEM, SMEM, VMEM, VMEM, VMEM],
        out_specs=VMEM,
        scratch_shapes=[pltpu.VMEM((sources * rows_own, 128), jnp.float32)],
        compiler_params=pltpu.CompilerParams(vmem_limit_bytes=48 << 20),
        name="prompt",
    )(
        slot,
        count,
        all_q,
        prompt_keys.reshape(prompts, positions, head_dim),
        prompt_values.reshape(prompts, positions, head_dim),
    )

    fresh = jnp.transpose(new_kv[:, :, :, 0, :], (0, 2, 1, 3))
    fresh = jnp.pad(fresh, ((0, 0), (0, 0), (0, PACK - steps), (0, 0)))
    wide = jax.ShapeDtypeStruct((rows_own * per_row, head_dim), jnp.float32)
    own = pl.pallas_call(
        functools.partial(own_kernel, per_row, steps, scale),
        out_shape=[wide, wide, wide],
        in_specs=[SMEM, VMEM, VMEM, VMEM],
        out_specs=[VMEM] * 3,
        compiler_params=pltpu.CompilerParams(vmem_limit_bytes=32 << 20),
        name="own",
    )(suffix_lengths, own_q, suffix_kv[:, :, :, 0, :], fresh)

    received = lax.all_to_all(partial, "seq", 0, 0)
    attention = pl.pallas_call(
        functools.partial(merge_kernel, per_row),
        out_shape=jax.ShapeDtypeStruct((rows_own * per_row, head_dim), jnp.bfloat16),
        in_specs=[VMEM] * 4,
        out_specs=VMEM,
        compiler_params=pltpu.CompilerParams(vmem_limit_bytes=32 << 20),
        name="merge",
    )(received, *own)
    attention = attention.reshape(rows_own * steps, heads_own * head_dim)
    attention_all = gather_seq(attention).reshape(-1, heads_own * head_dim)

    vocab_own = embedding.shape[0]
    local_ids = token_ids.reshape(-1) - lax.axis_index("head") * vocab_own
    inside = (local_ids >= 0) & (local_ids < vocab_own)
    embedded = jnp.take(embedding, jnp.clip(local_ids, 0, vocab_own - 1), axis=0)
    embedded = jnp.where(inside[:, None], embedded.astype(jnp.float32), 0.0)
    projected = jnp.dot(attention_all, out_weight, preferred_element_type=jnp.float32)
    terms = (projected + embedded).astype(jnp.bfloat16)
    heads = lax.axis_size("head")
    terms = lax.all_to_all(terms.reshape(heads, -1, terms.shape[1]), "head", 0, 0)
    hidden = jnp.sum(terms.astype(jnp.float32), axis=0).astype(jnp.bfloat16)
    return hidden.reshape(-1, steps, hidden.shape[1])


def solution(mesh):
    return jax.shard_map(
        shards,
        mesh=mesh,
        in_specs=(
            P(None, "seq", "head", None),
            P(None, None, "seq", "head", None),
            P(None, "seq", "head", None),
            P(None, "seq", "head", None),
            P(None, "seq", None, "head", None),
            P("seq", None),
            P("seq"),
            P(),
            P("head", "seq"),
            P("head", "seq"),
        ),
        out_specs=P("head", None, "seq"),
        check_vma=False,
    )
```

time: 745 us -> 215 us (0.29)
  waiting for transfers between devices: 277 us -> 61.9 us
  blocking collectives: 247 us -> 88.5 us
  local copies, waits for them, and re-layouts: 86.3 us -> 15.3 us
  matrix products: 55.2 us -> 1.06 us
  other arithmetic: 36.6 us -> 2.85 us
  Pallas kernels: 0 us -> 33.4 us
  loops' own time: 23.7 us -> 0 us
  between operations: 14.7 us -> 0.21 us
  starting transfers between devices: 0.13 us -> 11.2 us
    reduce_scatter x2 -> x0, waiting for transfers between devices: 153 us -> none  [the longest x1 121 us: shards(): lax.psum_scatter((blended * factor[..., None]).astype(jnp.bfloat16), 'seq...]
    all_gather x2 -> x0, waiting for transfers between devices: 123 us -> none  [the longest x1 71.4 us: shards(): attention_all = lax.all_gather(attention, 'seq', axis=0, tiled=True)]
    pmax x1 -> x0, blocking collectives: 115 us -> none  [shards(): lax.pmax(highest.astype(jnp.bfloat16), 'seq').astype(highest.dtype)]
    unnamed x1 -> x0, blocking collectives: 112 us -> none
    all_to_all x0 -> x4, blocking collectives: none -> 88.5 us  [the longest x3 69.7 us: spread(): lax.all_to_all(jnp.broadcast_to(x[None], (n,) + x.shape), 'seq', 0, 0, ax...]
    all_to_all x0 -> x2, waiting for transfers between devices: none -> 61.9 us  [the longest x1 46.8 us: shards(): received = lax.all_to_all(partial, 'seq', 0, 0)]
    dot_general x27 -> x1, matrix products: 55.2 us -> 1.06 us  [shards(): jnp.dot(attention_all, out_weight, preferred_element_type=jnp.float32)]
    dynamic_update_slice x22 -> x0, local copies, waits for them, and re-layouts: 34.1 us -> none  [the longest x11 17.2 us: per_tile(): lax.dynamic_update_slice_in_dim(peak_acc, jnp.where(flag, peak, old_peak)...]
  transfers between devices with their start and end apart: 4 -> 2, of which waited for: 4 -> 2; matrix products, arithmetic and copies ran while one was open for 2% -> 3% of each run, Pallas kernels for 0% -> 1%
where the time goes in v1:
time: 215 us
  blocking collectives  88.5 us (41%)
  waiting for transfers between devices  61.9 us (29%)
  Pallas kernels  33.4 us (16%)
  local copies, waits for them, and re-layouts  15.3 us (7%)
  starting transfers between devices  11.2 us (5%)
  other arithmetic  2.85 us (1%)
    all_to_all x3, blocking collectives, spread(): lax.all_to_all(jnp.broadcast_to(x[None], (n,) + x.shape), 'seq', 0, 0, ax...  69.7 us
    all_to_all x1, waiting for transfers between devices, shards(): received = lax.all_to_all(partial, 'seq', 0, 0)  46.8 us
    pallas_call x1, Pallas kernels, shards(): pl.pallas_call(functools.partial(prompt_kernel, per_row, scale), out_shap...  28.7 us
    all_to_all x1, blocking collectives, shards(): lax.all_to_all(terms.reshape(heads, -1, terms.shape[1]), 'head', 0, 0)  18.8 us
    all_to_all x1, waiting for transfers between devices, spread(): lax.all_to_all(jnp.broadcast_to(x[None], (n,) + x.shape), 'seq', 0, 0, ax...  15.1 us
    gather x1, local copies, waits for them, and re-layouts, shards(): jnp.take(embedding, jnp.clip(local_ids, 0, vocab_own - 1), axis=0)  6.19 us
    all_to_all x1, starting transfers between devices, shards(): received = lax.all_to_all(partial, 'seq', 0, 0)  5.73 us
    all_to_all x1, starting transfers between devices, spread(): lax.all_to_all(jnp.broadcast_to(x[None], (n,) + x.shape), 'seq', 0, 0, ax...  5.49 us
  transfers between devices with their start and end apart: 2, of which 2 were waited for; matrix products, arithmetic and copies ran while one was open for 3% of the time, Pallas kernels for 1%

profile of v1, /device:TPU:1, one launch (start us, length us, event | category | flops | bytes accessed | tf_op | source)
XLA Modules:
  0.0 214.5 jit_solution(9412937643418332262)
XLA Ops:
  0.0 0.0 copy-start
  0.0 0.9 copy.18
  0.9 0.7 convert_bitcast_fusion
  1.6 0.1 pad.7.clone
  1.7 0.1 maximum_maximum_fusion
  1.8 0.1 broadcast_in_dim.110
  1.9 25.3 %all_to_all.30 = bf16[8,272,128]{2,1,0:T(8,128)(2,1)S(1)} all-to-all(bf16[8,272,128]{2,1,0:T(8,128)(2,1)S(1)} %broadcast_in_dim.110), channel_id=1, replica_groups={{0,8,16,24,32,40,48,56},{64,72,80,88,96,104,112,120},{128,136,144,152,1..., dimensions={0} | all-to-all | bytes 1114112 | tf_op jit(solution)/shard_map/all_to_all | solution.py:154
  27.2 0.3 broadcast_in_dim.111
  27.5 0.0 copy-start.1
  27.5 28.7 %all_to_all.31 = bf16[4,8,272,128]{3,2,1,0:T(8,128)(2,1)S(1)} all-to-all(bf16[4,8,272,128]{3,2,1,0:T(8,128)(2,1)S(1)} %broadcast_in_dim.111), channel_id=1, replica_groups={{0,64,128,192},{8,72,136,200},{16,80,144,208},{24,88,152,216},{32,96,16..., dimensions={0} | all-to-all | bytes 4456448 | tf_op jit(solution)/shard_map/all_to_all | solution.py:154
  56.2 0.0 copy-start.5
  56.2 1.4 copy-done.5
  57.6 0.6 convert_reduce_fusion.1
  58.2 0.1 reshape.134
  58.3 0.1 convert_reduce_fusion.2
  58.4 0.2 convert_reduce_fusion
  58.6 0.6 fusion.3
  59.2 0.1 select_reduce_fusion.2
  59.4 0.1 select_reduce_fusion.1
  59.5 0.2 select_reduce_fusion
  59.6 0.0 copy-done.1
  59.6 0.0 copy-start.2
  59.6 1.6 copy-done.2
  61.2 28.7 %prompt.1 = bf16[32,272,128]{2,1,0:T(8,128)(2,1)} custom-call(s32[320]{0:T(512)S(1)} %add_select_fusion.slot_ref, s32[1]{0:T(128)} %bitcast.4.count_ref, bf16[32,272,128]{2,1,0:T(8,128)(2,1)} %bitcast.25, bf16[8,1024,128]{2,1,0:T(8,128)(2,1)S(1)} %bitcast.19, bf16[8,1024,128]{2,1,0:T(8,128)(2,1)S(1)} %bitcast.20), custom_call_target="tpu_custom_call" | custom-call | tf_op jit(solution)/shard_map/prompt/pallas_call | solution.py:190
  89.9 0.0 copy-start.6
  89.9 0.0 copy-start.4
  89.9 5.7 %all-to-all-start.2 = ((bf16[32,272,128]{2,1,0:T(8,128)(2,1)}), bf16[32,272,128]{2,1,0:T(8,128)(2,1)S(1)}, u32[]{:S(2)}, u32[]{:S(2)}) async-start(bf16[32,272,128]{2,1,0:T(8,128)(2,1)} %prompt.1), calls=%async_computation.2 | async-start | bytes 4456448 | tf_op jit(solution)/shard_map/all_to_all | solution.py:218
  95.7 0.0 copy-done.6
  95.7 0.0 copy-done.4
  95.7 0.0 copy-start.3
  95.8 1.6 copy-done.3
  97.3 2.7 %own.1 = (f32[256,128]{1,0:T(8,128)S(1)}, f32[256,128]{1,0:T(8,128)S(1)}, f32[256,128]{1,0:T(8,128)S(1)}) custom-call(s32[8]{0:T(128)S(1)} %copy-done.4, bf16[256,128]{1,0:T(8,128)(2,1)S(1)} %bitcast.23, bf16[2,8,512,128]{3,2,1,0:T(8,128)(2,1)S(1)} %bitcast.21, bf16[2,8,16,128]{3,2,1,0:T(8,128)(2,1)S(1)} %pad.4.fresh_ref), custom_call_target="tpu_custom_call" | custom-call | tf_op jit(solution)/shard_map/own/pallas_call | solution.py:209
  100.1 46.8 %all-to-all-done.2.parts_ref = bf16[32,272,128]{2,1,0:T(8,128)(2,1)S(1)} async-done(((bf16[32,272,128]{2,1,0:T(8,128)(2,1)}), bf16[32,272,128]{2,1,0:T(8,128)(2,1)S(1)}, u32[]{:S(2)}, u32[]{:S(2)}) %all-to-all-start.2) | async-done | bytes 2228256 | tf_op jit(solution)/shard_map/all_to_all | solution.py:218
  146.9 2.0 merge.1
  148.9 0.1 broadcast_in_dim.119
  149.0 15.7 %all_to_all.32 = bf16[8,32,1024]{2,1,0:T(8,128)(2,1)S(1)} all-to-all(bf16[8,32,1024]{2,1,0:T(8,128)(2,1)S(1)} %broadcast_in_dim.119), channel_id=1, replica_groups={{0,8,16,24,32,40,48,56},{64,72,80,88,96,104,112,120},{128,136,144,152,1..., dimensions={0} | all-to-all | bytes 1048576 | tf_op jit(solution)/shard_map/all_to_all | solution.py:154
  164.7 1.6 broadcast_in_dim.120
  166.3 0.0 copy-start.7
  166.3 5.5 %all-to-all-start.4 = ((bf16[4,8,32,1024]{3,2,1,0:T(8,128)(2,1)}), bf16[4,8,32,1024]{3,2,1,0:T(8,128)(2,1)S(1)}, u32[]{:S(2)}, u32[]{:S(2)}) async-start(bf16[4,8,32,1024]{3,2,1,0:T(8,128)(2,1)} %broadcast_in_dim.120), calls=%async_computation.4 | async-start | bytes 4194304 | tf_op jit(solution)/shard_map/all_to_all | solution.py:154
  171.8 0.0 copy-done.7
  171.8 0.1 copy.21
  171.9 0.1 min.18
  172.1 0.1 min.16
  172.2 0.2 copy.20
  172.4 0.1 and.43
  172.6 6.2 %gather_fusion = bf16[1024,256]{1,0:T(8,128)(2,1)S(1)} fusion(bf16[8192,256]{1,0:T(8,128)(2,1)} %param.18, s32[1024]{0:T(1024)S(1)} %broadcast_clamp_fusion), kind=kCustom, calls=%fused_computation | custom fusion | bytes 1052672 | tf_op jit(solution)/shard_map/jit(_take)/gather | solution.py:233
  178.8 15.1 %all-to-all-done.4 = bf16[4,8,32,1024]{3,2,1,0:T(8,128)(2,1)S(1)} async-done(((bf16[4,8,32,1024]{3,2,1,0:T(8,128)(2,1)}), bf16[4,8,32,1024]{3,2,1,0:T(8,128)(2,1)S(1)}, u32[]{:S(2)}, u32[]{:S(2)}) %all-to-all-start.4) | async-done | bytes 2097184 | tf_op jit(solution)/shard_map/all_to_all | solution.py:154
  193.9 0.0 copy-done
  193.9 1.1 fusion
  194.9 18.8 %all_to_all.33 = bf16[8,128,256]{2,1,0:T(8,128)(2,1)S(1)} all-to-all(bf16[8,128,256]{2,1,0:T(8,128)(2,1)S(1)} %bitcast.27), channel_id=1, replica_groups=mesh['seq'=32,'head'=8] {'head'}, dimensions={0} | all-to-all | bytes 1048576 | tf_op jit(solution)/shard_map/all_to_all | solution.py:238
  213.8 0.1 reduce_sum.62
  213.9 0.7 reshape.133
  (13 shorter events, 0.1 us)
Async XLA Ops:
  0.0 193.9 %copy-start = (bf16[1024,256]{1,0:T(8,128)(2,1)S(1)}, bf16[1024,256]{1,0:T(8,128)(2,1)}, u32[]{:S(2)}) copy-start(bf16[1024,256]{1,0:T(8,128)(2,1)} %param.19) | copy-start | bytes 1572868
  27.5 32.2 %copy-start.1 = (bf16[8,1024,1,128]{3,1,2,0:T(8,128)(2,1)S(1)}, bf16[8,1024,1,128]{3,1,2,0:T(8,128)(2,1)}, u32[]{:S(2)}) copy-start(bf16[8,1024,1,128]{3,1,2,0:T(8,128)(2,1)} %param.12) | copy-start | bytes 6291460
  56.2 1.4 copy-start.5
  59.6 1.6 copy-start.2
  89.9 5.7 %copy-start.6 = (bf16[2,4,8,1,128]{4,2,3,1,0:T(8,128)(2,1)S(1)}, bf16[2,4,8,1,128]{4,2,3,1,0:T(8,128)(2,1)}, u32[]{:S(2)}) copy-start(bf16[2,4,8,1,128]{4,2,3,1,0:T(8,128)(2,1)} %param.11) | copy-start | bytes 49156
  89.9 5.8 %copy-start.4 = (s32[8]{0:T(128)S(1)}, s32[8]{0:T(128)}, u32[]{:S(2)}) copy-start(s32[8]{0:T(128)} %len_ref.1) | copy-start | bytes 100
  89.9 56.9 %all-to-all-start.2 = ((bf16[32,272,128]{2,1,0:T(8,128)(2,1)}), bf16[32,272,128]{2,1,0:T(8,128)(2,1)S(1)}, u32[]{:S(2)}, u32[]{:S(2)}) async-start(bf16[32,272,128]{2,1,0:T(8,128)(2,1)} %prompt.1), calls=%async_computation.2 | async-start | bytes 4456448 | tf_op jit(solution)/shard_map/all_to_all | solution.py:218
  95.7 1.6 copy-start.3
  166.3 5.5 %copy-start.7 = (s32[256,4]{0,1:T(4,128)S(1)}, s32[256,4]{0,1:T(4,128)}, u32[]{:S(2)}) copy-start(s32[256,4]{0,1:T(4,128)} %param.17) | copy-start | bytes 12292
  166.3 27.6 %all-to-all-start.4 = ((bf16[4,8,32,1024]{3,2,1,0:T(8,128)(2,1)}), bf16[4,8,32,1024]{3,2,1,0:T(8,128)(2,1)S(1)}, u32[]{:S(2)}, u32[]{:S(2)}) async-start(bf16[4,8,32,1024]{3,2,1,0:T(8,128)(2,1)} %broadcast_in_dim.120), calls=%async_computation.4 | async-start | bytes 4194304 | tf_op jit(solution)/shard_map/all_to_all | solution.py:154

commit v2 on v1

v2 whole, which is shorter than its diff:
```python
import functools
import math

import jax
import jax.numpy as jnp
from jax import lax
from jax.experimental import pallas as pl
from jax.experimental.pallas import tpu as pltpu
from jax.sharding import PartitionSpec as P

BLOCK_ROWS = 4
DEPTH = 2
OWNER_ROWS = 8
PACK = 16
LOG2E = 1.0 / math.log(2.0)
SEQ_X, SEQ_Z = 4, 8
Z_GROUPS = [[x * SEQ_Z + z for z in range(SEQ_Z)] for x in range(SEQ_X)]
X_GROUPS = [[x * SEQ_Z + z for x in range(SEQ_X)] for z in range(SEQ_Z)]
VMEM = pl.BlockSpec(memory_space=pltpu.VMEM)
SMEM = pl.BlockSpec(memory_space=pltpu.SMEM)
HBM = pl.BlockSpec(memory_space=pltpu.HBM)


def three_terms(x):
    hi = x.astype(jnp.bfloat16).astype(jnp.float32)
    mid = (x - hi).astype(jnp.bfloat16).astype(jnp.float32)
    return hi, mid, (x - hi) - mid


def in_hbm(x):
    return pltpu.with_memory_space_constraint(x, pltpu.HBM)


def slot_table(rows, prompts, ids_ref, slot_ref, next_ref):
    for p in range(prompts):
        next_ref[p] = 0

    def count(r, carry):
        p = ids_ref[r // OWNER_ROWS, r % OWNER_ROWS]
        next_ref[p] = next_ref[p] + 1
        return carry

    def place(r, carry):
        p = ids_ref[r // OWNER_ROWS, r % OWNER_ROWS]
        k = next_ref[p]
        slot_ref[k] = r * prompts + p
        next_ref[p] = k + 1
        return carry

    lax.fori_loop(0, rows, count, 0, unroll=True)
    end = jnp.int32(0)
    ends = []
    for p in range(prompts):
        need = (next_ref[p] + BLOCK_ROWS - 1) // BLOCK_ROWS * BLOCK_ROWS
        next_ref[p] = end
        end = end + need
        ends.append(end)
    lax.fori_loop(0, rows, place, 0, unroll=True)
    for p in range(prompts):
        filled = next_ref[p]
        last = slot_ref[jnp.maximum(filled - 1, 0)]
        for i in range(BLOCK_ROWS - 1):

            @pl.when(filled + i < ends[p])
            def _():
                slot_ref[filled + i] = last

    return end // BLOCK_ROWS


def prompt_kernel(
    per_row,
    scale,
    q_ref,
    k_hbm,
    v_hbm,
    out_ref,
    k_ref,
    v_ref,
    stat_ref,
    score_ref,
    slot_ref,
    next_ref,
    held_ref,
    ids_ref,
    ids_sem,
    k_sem,
    v_sem,
):
    owners = out_ref.shape[0]
    prompts = k_ref.shape[0]
    queries = BLOCK_ROWS * per_row
    body_rows = OWNER_ROWS * per_row
    def load(p):
        return (
            pltpu.make_async_copy(k_hbm.at[p], k_ref.at[p], k_sem.at[p]),
            pltpu.make_async_copy(v_hbm.at[p], v_ref.at[p], v_sem.at[p]),
        )

    def finish(p, carry):
        for copy in load(p):
            copy.wait()
        return carry

    held_ref[...] = q_ref[:, body_rows, :].astype(jnp.float32).astype(jnp.int32)
    ids_copy = pltpu.make_async_copy(held_ref, ids_ref, ids_sem)
    ids_copy.start()
    for p in range(prompts):
        for copy in load(p):
            copy.start()
    ids_copy.wait()
    blocks = slot_table(owners * OWNER_ROWS, prompts, ids_ref, slot_ref, next_ref)

    def locate(b):
        codes = [slot_ref[b * BLOCK_ROWS + j] for j in range(BLOCK_ROWS)]
        rows = [code // prompts for code in codes]
        where = [
            (r // OWNER_ROWS, pl.ds(pl.multiple_of(r % OWNER_ROWS * per_row, per_row), per_row))
            for r in rows
        ]
        return rows, where, codes[0] % prompts

    def score(b, at):
        _, where, prompt = locate(b)
        q = jnp.concatenate([q_ref[o, w, :] for o, w in where], axis=0)
        score_ref[at] = lax.dot_general(
            q, k_ref[prompt], (((1,), (1,)), ((), ())), preferred_element_type=jnp.float32
        )

    def mix(b, at):
        rows, where, prompt = locate(b)
        s = score_ref[at]
        top = jnp.max(s, axis=-1, keepdims=True) * scale
        p = jnp.exp2(s * scale - top)
        total = jnp.sum(p, axis=-1, keepdims=True)
        mixed = jnp.dot(
            p.astype(jnp.bfloat16), v_ref[prompt], preferred_element_type=jnp.float32
        )
        mixed = (mixed / total).astype(jnp.bfloat16)
        hi, mid, lo = three_terms(top)
        lane = lax.broadcasted_iota(jnp.int32, (queries, 128), 1)
        at_row = lax.broadcasted_iota(jnp.int32, (queries, 128), 0) % per_row
        part = lane // per_row
        stat = jnp.where(part == 0, hi, jnp.where(part == 1, mid, jnp.where(part == 2, lo, total)))
        stat = jnp.where(lane % per_row == at_row, stat, 0.0)
        stat = jnp.sum(stat.reshape(BLOCK_ROWS, per_row, 128), axis=1)
        return rows, where, mixed, stat

    def put(rows, where, mixed, stat):
        for j in range(BLOCK_ROWS):
            o, w = where[j]
            out_ref[o, w, :] = mixed[j * per_row : (j + 1) * per_row, :]
            stat_ref[pl.ds(rows[j], 1), :] = stat[j : j + 1, :]

    def clip(b):
        return jnp.minimum(b, blocks - 1)

    def ready(b, waited):
        end = slot_ref[clip(b) * BLOCK_ROWS] % prompts + 1
        lax.fori_loop(waited, end, finish, 0)
        return jnp.maximum(waited, end)

    waited = ready(DEPTH - 1, jnp.int32(0))
    for u in range(DEPTH):
        score(clip(u), u)

    def sweep(i, waited):
        first = i * 2 * DEPTH
        waited = ready(first + 3 * DEPTH - 1, waited)
        for half in range(2):
            here, there = half * DEPTH, (1 - half) * DEPTH
            done = [mix(clip(first + here + u), here + u) for u in range(DEPTH)]
            for u in range(DEPTH):
                score(clip(first + here + DEPTH + u), there + u)
            for d in done:
                put(*d)
        return waited

    waited = lax.fori_loop(0, (blocks + 2 * DEPTH - 1) // (2 * DEPTH), sweep, waited)
    lax.fori_loop(waited, prompts, finish, 0)
    for o in range(owners):
        out_ref[o, body_rows : body_rows + PACK, :] = padded(
            stat_ref[o * OWNER_ROWS : (o + 1) * OWNER_ROWS, :]
        )


def padded(stat):
    pad = jnp.zeros((PACK - OWNER_ROWS, stat.shape[1]), jnp.float32)
    return jnp.concatenate([stat, pad], axis=0).astype(jnp.bfloat16)


def read_stats(per_row, ref_part):
    stat = ref_part.astype(jnp.float32)[:, :OWNER_ROWS, :]
    n = stat.shape[0]
    stat = stat.reshape(n * OWNER_ROWS, 128)
    top = (
        stat + pltpu.roll(stat, 128 - per_row, 1) + pltpu.roll(stat, 128 - 2 * per_row, 1)
    )
    total = pltpu.roll(stat, 128 - 3 * per_row, 1)
    return top.reshape(n, OWNER_ROWS, 128), total.reshape(n, OWNER_ROWS, 128)


def join_kernel(per_row, *refs):
    parts, out_ref = refs[:-1], refs[-1]
    n = len(parts)
    body_rows = OWNER_ROWS * per_row
    lane = lax.broadcasted_iota(jnp.int32, (OWNER_ROWS, 128), 1) // per_row
    for o in range(out_ref.shape[0]):
        stats = [read_stats(per_row, ref[o : o + 1, body_rows : body_rows + PACK, :]) for ref in parts]
        tops = [t[0] for t, _ in stats]
        peak = functools.reduce(jnp.maximum, tops)
        weights = [total[0] * jnp.exp2(t - peak) for t, (_, total) in zip(tops, stats)]
        summed = functools.reduce(jnp.add, weights)
        table = jnp.concatenate([w / summed for w in weights], axis=0)
        table = jnp.transpose(table)[:per_row, :]
        for j in range(OWNER_ROWS):
            span = slice(j * per_row, (j + 1) * per_row)
            acc = jnp.zeros((per_row, 128), jnp.float32)
            for i in range(n):
                at = i * OWNER_ROWS + j
                acc += table[:, at : at + 1] * parts[i][o, span, :].astype(jnp.float32)
            out_ref[o, span, :] = acc.astype(jnp.bfloat16)
        hi, mid, lo = three_terms(peak)
        stat = jnp.where(
            lane == 0,
            hi,
            jnp.where(
                lane == 1,
                pltpu.roll(mid, per_row, 1),
                jnp.where(
                    lane == 2, pltpu.roll(lo, 2 * per_row, 1), pltpu.roll(summed, 3 * per_row, 1)
                ),
            ),
        )
        out_ref[o, body_rows : body_rows + PACK, :] = padded(stat)


def own_kernel(per_row, steps, scale, len_ref, q_ref, kv_ref, fresh_ref, out_ref, top_ref, total_ref):
    rows, length = kv_ref.shape[1], kv_ref.shape[2]
    group = per_row // steps
    pos = lax.broadcasted_iota(jnp.int32, (per_row, length), 1)
    step_of = lax.broadcasted_iota(jnp.int32, (per_row, PACK), 0) // group
    fresh_at = lax.broadcasted_iota(jnp.int32, (per_row, PACK), 1)
    over_last = (((1,), (1,)), ((), ()))
    for j in range(rows):
        part = pl.ds(j * per_row, per_row)
        q = q_ref[part, :]
        s = lax.dot_general(q, kv_ref[0, j], over_last, preferred_element_type=jnp.float32)
        s = jnp.where(pos < len_ref[j], s * scale, -jnp.inf)
        f = lax.dot_general(q, fresh_ref[0, j], over_last, preferred_element_type=jnp.float32)
        f = jnp.where(fresh_at <= step_of, f * scale, -jnp.inf)
        top = jnp.maximum(
            jnp.max(s, axis=-1, keepdims=True), jnp.max(f, axis=-1, keepdims=True)
        )
        ps, pf = jnp.exp2(s - top), jnp.exp2(f - top)
        total = jnp.sum(ps, axis=-1, keepdims=True) + jnp.sum(pf, axis=-1, keepdims=True)
        mixed = jnp.dot(ps.astype(jnp.bfloat16), kv_ref[1, j], preferred_element_type=jnp.float32)
        mixed += jnp.dot(
            pf.astype(jnp.bfloat16), fresh_ref[1, j], preferred_element_type=jnp.float32
        )
        out_ref[part, :] = mixed
        top_ref[part, :] = jnp.broadcast_to(top, (per_row, 128))
        total_ref[part, :] = jnp.broadcast_to(total, (per_row, 128))


def project_kernel(chip_ref, *refs):
    tokens_ref, weights, out_ref = refs[0], refs[1:-1], refs[-1]
    slots = out_ref.shape[0]
    for t, weight in enumerate(weights):
        out_ref[(chip_ref[0] + slots - t) % slots] = jnp.dot(
            tokens_ref[...], weight[...], preferred_element_type=jnp.float32
        ).astype(jnp.bfloat16)


def merge_kernel(per_row, parts_ref, own_ref, top_ref, total_ref, out_ref):
    sources = parts_ref.shape[0]
    rows = OWNER_ROWS
    top, total = read_stats(per_row, parts_ref[:, rows * per_row : rows * per_row + PACK, :])
    peak = jnp.max(top, axis=0)
    weight = total * jnp.exp2(top - peak[None])
    summed = jnp.sum(weight, axis=0)
    for j in range(rows):
        table = jnp.concatenate(
            [weight[:, j, :], peak[j : j + 1, :], summed[j : j + 1, :], jnp.zeros((6, 128), jnp.float32)],
            axis=0,
        )
        table = jnp.transpose(table)[:per_row, :]
        span = slice(j * per_row, (j + 1) * per_row)
        acc = jnp.zeros((per_row, 128), jnp.float32)
        for i in range(sources):
            acc += table[:, i : i + 1] * parts_ref[i, span, :].astype(jnp.float32)
        prompt_top = table[:, sources : sources + 1]
        prompt_sum = table[:, sources + 1 : sources + 2]
        own_top = top_ref[span, :]
        best = jnp.maximum(prompt_top, own_top)
        a, b = jnp.exp2(prompt_top - best), jnp.exp2(own_top - best)
        num = acc * a + own_ref[span, :] * b
        den = prompt_sum * a + total_ref[span, :] * b
        out_ref[span, :] = (num / den).astype(jnp.bfloat16)


def spread(x, groups):
    n = len(groups[0])
    return lax.all_to_all(
        jnp.broadcast_to(x[None], (n,) + x.shape), "seq", 0, 0, axis_index_groups=groups
    )


def shift_x(x, by):
    pairs = [
        (i * SEQ_Z + z, (i + by) % SEQ_X * SEQ_Z + z) for i in range(SEQ_X) for z in range(SEQ_Z)
    ]
    return lax.ppermute(x, "seq", pairs)


def shards(
    queries,
    new_kv,
    prompt_keys,
    prompt_values,
    suffix_kv,
    prompt_ids,
    suffix_lengths,
    token_ids,
    embedding,
    out_weight,
):
    steps, rows_own, heads_own, head_dim = queries.shape
    prompts, positions = prompt_keys.shape[0], prompt_keys.shape[1]
    per_row = steps * heads_own
    scale = head_dim ** (-0.5) * LOG2E
    own_q = jnp.transpose(queries, (1, 0, 2, 3)).reshape(rows_own * per_row, head_dim)
    ids = jnp.pad(
        prompt_ids.reshape(1, rows_own).astype(jnp.bfloat16),
        ((0, PACK - 1), (0, head_dim - rows_own)),
    )
    packed = jnp.concatenate([own_q, ids])
    row_q = spread(packed, Z_GROUPS)
    owners = row_q.shape[0]
    chunk_rows = owners * rows_own
    blocks = chunk_rows // BLOCK_ROWS + prompts
    payload = jax.ShapeDtypeStruct(row_q.shape, jnp.bfloat16)
    keys = in_hbm(prompt_keys.reshape(prompts, positions, head_dim))
    values = in_hbm(prompt_values.reshape(prompts, positions, head_dim))
    pairs = chunk_rows * per_row * positions
    attend = pl.pallas_call(
        functools.partial(prompt_kernel, per_row, scale),
        out_shape=payload,
        in_specs=[VMEM, HBM, HBM],
        out_specs=VMEM,
        scratch_shapes=[
            pltpu.VMEM(keys.shape, jnp.bfloat16),
            pltpu.VMEM(values.shape, jnp.bfloat16),
            pltpu.VMEM((chunk_rows, 128), jnp.float32),
            pltpu.VMEM((2 * DEPTH, BLOCK_ROWS * per_row, positions), jnp.float32),
            pltpu.SMEM((blocks * BLOCK_ROWS,), jnp.int32),
            pltpu.SMEM((prompts,), jnp.int32),
            pltpu.VMEM((owners, 128), jnp.int32),
            pltpu.SMEM((owners, 128), jnp.int32),
            pltpu.SemaphoreType.DMA(()),
            pltpu.SemaphoreType.DMA((prompts,)),
            pltpu.SemaphoreType.DMA((prompts,)),
        ],
        compiler_params=pltpu.CompilerParams(vmem_limit_bytes=24 << 20),
        cost_estimate=pl.CostEstimate(
            flops=8 * pairs * head_dim, bytes_accessed=4 << 20, transcendentals=pairs
        ),
        name="prompt",
    )

    def partial_of(q):
        return attend(q, keys, values)

    turns = [1, SEQ_X - 1, 2]
    arrived = [shift_x(row_q, t) for t in turns]
    first, arrived[0] = lax.optimization_barrier((partial_of(row_q), arrived[0]))
    partials = [first]
    partials += [shift_x(partial_of(q), -t) for q, t in zip(arrived, turns)]
    joined = pl.pallas_call(
        functools.partial(join_kernel, per_row),
        out_shape=payload,
        in_specs=[VMEM] * len(partials),
        out_specs=VMEM,
        compiler_params=pltpu.CompilerParams(vmem_limit_bytes=32 << 20),
        name="join",
    )(*partials)
    fresh = jnp.transpose(new_kv[:, :, :, 0, :], (0, 2, 1, 3))
    fresh = jnp.pad(fresh, ((0, 0), (0, 0), (0, PACK - steps), (0, 0)))
    wide = jax.ShapeDtypeStruct((rows_own * per_row, head_dim), jnp.float32)
    own = pl.pallas_call(
        functools.partial(own_kernel, per_row, steps, scale),
        out_shape=[wide, wide, wide],
        in_specs=[SMEM, VMEM, VMEM, VMEM],
        out_specs=[VMEM] * 3,
        compiler_params=pltpu.CompilerParams(vmem_limit_bytes=32 << 20),
        name="own",
    )(suffix_lengths, own_q, suffix_kv[:, :, :, 0, :], fresh)

    joined, weight = lax.optimization_barrier((joined, out_weight))
    near = [shift_x(weight, 1), shift_x(weight, 3)]
    received = lax.all_to_all(joined, "seq", 0, 0, axis_index_groups=Z_GROUPS)
    vocab_own = embedding.shape[0]
    local_ids = token_ids.reshape(-1) - lax.axis_index("head") * vocab_own
    inside = (local_ids >= 0) & (local_ids < vocab_own)
    embedded = jnp.take(embedding, jnp.clip(local_ids, 0, vocab_own - 1), axis=0)
    embedded = jnp.where(inside[:, None], embedded, jnp.zeros_like(embedded))
    received, embedded, *near = lax.optimization_barrier((received, embedded, *near))
    attention = pl.pallas_call(
        functools.partial(merge_kernel, per_row),
        out_shape=jax.ShapeDtypeStruct((rows_own * per_row, head_dim), jnp.bfloat16),
        in_specs=[VMEM] * 4,
        out_specs=VMEM,
        compiler_params=pltpu.CompilerParams(vmem_limit_bytes=32 << 20),
        name="merge",
    )(received, *own)
    attention = attention.reshape(rows_own * steps, heads_own * head_dim)
    attention, weight = lax.optimization_barrier((attention, weight))
    weights_x = [weight, near[0], shift_x(weight, 2), near[1]]
    attention_z = spread(attention, Z_GROUPS).reshape(-1, heads_own * head_dim)

    heads = lax.axis_size("head")
    chip = (lax.axis_index("seq") // SEQ_Z).astype(jnp.int32).reshape(1)
    projected = pl.pallas_call(
        project_kernel,
        out_shape=jax.ShapeDtypeStruct(
            (SEQ_X, attention_z.shape[0], out_weight.shape[1]), jnp.bfloat16
        ),
        in_specs=[SMEM] + [VMEM] * (1 + len(weights_x)),
        out_specs=VMEM,
        compiler_params=pltpu.CompilerParams(vmem_limit_bytes=24 << 20),
        name="project",
    )(chip, attention_z, *weights_x)
    projected = lax.all_to_all(projected, "seq", 0, 0, axis_index_groups=X_GROUPS)
    projected = projected.reshape(embedded.shape).astype(jnp.float32)
    terms = (projected + embedded.astype(jnp.float32)).astype(jnp.bfloat16)
    terms = lax.all_to_all(terms.reshape(heads, -1, terms.shape[1]), "head", 0, 0)
    hidden = jnp.sum(terms.astype(jnp.float32), axis=0).astype(jnp.bfloat16)
    return hidden.reshape(-1, steps, hidden.shape[1])


def solution(mesh):
    return jax.shard_map(
        shards,
        mesh=mesh,
        in_specs=(
            P(None, "seq", "head", None),
            P(None, None, "seq", "head", None),
            P(None, "seq", "head", None),
            P(None, "seq", "head", None),
            P(None, "seq", None, "head", None),
            P("seq", None),
            P("seq"),
            P(),
            P("head", "seq"),
            P("head", "seq"),
        ),
        out_specs=P("head", None, "seq"),
        check_vma=False,
    )
```

time: 215 us -> 162 us (0.75)
  waiting for transfers between devices: 61.9 us -> 26.5 us
  blocking collectives: 88.5 us -> 55.8 us
  starting transfers between devices: 11.2 us -> 21.9 us
  Pallas kernels: 33.4 us -> 43.2 us
  local copies, waits for them, and re-layouts: 15.3 us -> 11.8 us
    all_to_all x1, waiting for transfers between devices: 46.8 us -> 0.25 us  [shards(): received = lax.all_to_all(joined, 'seq', 0, 0, axis_index_groups=Z_GROUPS)]
    all_to_all x3 -> x1, blocking collectives: 69.7 us -> 25.3 us  [spread(): lax.all_to_all(jnp.broadcast_to(x[None], (n,) + x.shape), 'seq', 0, 0, ax...]
    ppermute x0 -> x9, waiting for transfers between devices: none -> 24.1 us  [shift_x(): return lax.ppermute(x, 'seq', pairs)]
    all_to_all x1, waiting for transfers between devices: 15.1 us -> 2.2 us  [spread(): lax.all_to_all(jnp.broadcast_to(x[None], (n,) + x.shape), 'seq', 0, 0, ax...]
    pallas_call x1 -> x6, Pallas kernels: 28.7 us -> 39.8 us  [the longest x4 33.5 us: partial_of(): return attend(q, keys, values)]
    ppermute x0 -> x9, starting transfers between devices: none -> 10.4 us  [shift_x(): return lax.ppermute(x, 'seq', pairs)]
    all_to_all x0 -> x1, blocking collectives: none -> 9.33 us  [shards(): lax.all_to_all(projected, 'seq', 0, 0, axis_index_groups=X_GROUPS)]
    unnamed x17, local copies, waits for them, and re-layouts: 4.59 us -> 1.21 us
  transfers between devices with their start and end apart: 2 -> 11, of which waited for: 2 -> 5; matrix products, arithmetic and copies ran while one was open for 3% -> 5% of each run, Pallas kernels for 1% -> 23%
where the time goes in v2:
time: 162 us; the launch traced here: 161 us
  blocking collectives  55.8 us (34%)
  Pallas kernels  43.2 us (27%)
  waiting for transfers between devices  26.5 us (16%)
  starting transfers between devices  21.9 us (14%)
  local copies, waits for them, and re-layouts  11.8 us (7%)
    pallas_call x4, Pallas kernels, partial_of(): return attend(q, keys, values)  33.5 us
    all_to_all x1, blocking collectives, spread(): lax.all_to_all(jnp.broadcast_to(x[None], (n,) + x.shape), 'seq', 0, 0, ax...  25.3 us
    ppermute x9, waiting for transfers between devices, shift_x(): return lax.ppermute(x, 'seq', pairs)  24.1 us
    all_to_all x1, blocking collectives, shards(): lax.all_to_all(terms.reshape(heads, -1, terms.shape[1]), 'head', 0, 0)  21.2 us
    ppermute x9, starting transfers between devices, shift_x(): return lax.ppermute(x, 'seq', pairs)  10.4 us
    all_to_all x1, blocking collectives, shards(): lax.all_to_all(projected, 'seq', 0, 0, axis_index_groups=X_GROUPS)  9.33 us
    gather x1, local copies, waits for them, and re-layouts, shards(): jnp.take(embedding, jnp.clip(local_ids, 0, vocab_own - 1), axis=0)  7.46 us
    all_to_all x1, starting transfers between devices, spread(): lax.all_to_all(jnp.broadcast_to(x[None], (n,) + x.shape), 'seq', 0, 0, ax...  6.4 us
  transfers between devices with their start and end apart: 11, of which 5 were waited for; matrix products, arithmetic and copies ran while one was open for 5% of the time, Pallas kernels for 23%

profile of v2, /device:TPU:1, one launch (start us, length us, event | category | flops | bytes accessed | tf_op | source)
XLA Modules:
  0.0 160.8 jit_solution(16924369576084968968)
XLA Ops:
  0.0 0.7 convert_bitcast_fusion
  0.7 0.9 copy.13
  1.5 0.1 broadcast_in_dim.34
  1.6 25.3 %all_to_all.25.q_ref = bf16[8,272,128]{2,1,0:T(8,128)(2,1)S(1)} all-to-all(bf16[8,272,128]{2,1,0:T(8,128)(2,1)S(1)} %broadcast_in_dim.34), channel_id=1, replica_groups={{0,8,16,24,32,40,48,56},{64,72,80,88,96,104,112,120},{128,136,144,152,1..., dimensions={0} | all-to-all | bytes 1114112 | tf_op jit(solution)/shard_map/all_to_all | solution.py:304
  26.9 1.2 collective-permute-start
  28.1 1.5 collective-permute-start.2
  29.6 1.5 collective-permute-start.4
  31.1 7.7 %prompt.4.refs_0_ = bf16[8,272,128]{2,1,0:T(8,128)(2,1)S(1)} custom-call(bf16[8,272,128]{2,1,0:T(8,128)(2,1)S(1)} %all_to_all.25.q_ref, bf16[8,1024,128]{2,1,0:T(8,128)(2,1)} %bitcast.27, bf16[8,1024,128]{2,1,0:T(8,128)(2,1)} %bitcast.31), custom_call_target="tpu_custom_call" | custom-call | flops 2147483648 | bytes 4194304 | tf_op jit(solution)/shard_map/prompt/pallas_call | solution.py:372
  38.9 0.7 collective-permute-done.q_ref
  39.5 8.6 %prompt.5 = bf16[8,272,128]{2,1,0:T(8,128)(2,1)} custom-call(bf16[8,272,128]{2,1,0:T(8,128)(2,1)S(1)} %collective-permute-done.q_ref, bf16[8,1024,128]{2,1,0:T(8,128)(2,1)} %bitcast.28, bf16[8,1024,128]{2,1,0:T(8,128)(2,1)} %bitcast.32), custom_call_target="tpu_custom_call" | custom-call | flops 2147483648 | bytes 4194304 | tf_op jit(solution)/shard_map/prompt/pallas_call | solution.py:372
  48.1 1.4 collective-permute-start.1
  49.5 0.0 collective-permute-done.2.q_ref
  49.5 8.6 %prompt.6 = bf16[8,272,128]{2,1,0:T(8,128)(2,1)} custom-call(bf16[8,272,128]{2,1,0:T(8,128)(2,1)S(1)} %collective-permute-done.2.q_ref, bf16[8,1024,128]{2,1,0:T(8,128)(2,1)} %bitcast.29, bf16[8,1024,128]{2,1,0:T(8,128)(2,1)} %bitcast.33), custom_call_target="tpu_custom_call" | custom-call | flops 2147483648 | bytes 4194304 | tf_op jit(solution)/shard_map/prompt/pallas_call | solution.py:372
  58.1 0.0 copy-start.7
  58.1 0.3 collective-permute-start.3
  58.4 0.0 collective-permute-done.4.q_ref
  58.4 8.6 %prompt.7 = bf16[8,272,128]{2,1,0:T(8,128)(2,1)} custom-call(bf16[8,272,128]{2,1,0:T(8,128)(2,1)S(1)} %collective-permute-done.4.q_ref, bf16[8,1024,128]{2,1,0:T(8,128)(2,1)} %bitcast.30, bf16[8,1024,128]{2,1,0:T(8,128)(2,1)} %bitcast.34), custom_call_target="tpu_custom_call" | custom-call | flops 2147483648 | bytes 4194304 | tf_op jit(solution)/shard_map/prompt/pallas_call | solution.py:372
  67.0 1.8 %collective-permute-start.5 = (bf16[8,272,128]{2,1,0:T(8,128)(2,1)}, bf16[8,272,128]{2,1,0:T(8,128)(2,1)S(1)}, u32[]{:S(2)}, u32[]{:S(2)}) collective-permute-start(bf16[8,272,128]{2,1,0:T(8,128)(2,1)} %prompt.7), channel_id=1, source_target_pairs={{0,128},{8,136},{16,144},{24,152},{32,160},{40,168},{48,176},{56,1... | collective-permute-start | bytes 1671176 | tf_op jit(solution)/shard_map/ppermute | solution.py:313
  68.8 0.0 copy-done.7
  68.8 0.0 copy-start.1
  68.8 0.1 copy.15
  69.0 0.0 copy-start.6
  69.0 0.1 min.18
  69.1 0.0 collective-permute-done.1.refs_1_
  69.1 0.0 collective-permute-done.3.refs_2_
  69.1 13.6 %collective-permute-done.5.refs_3_ = bf16[8,272,128]{2,1,0:T(8,128)(2,1)S(1)} collective-permute-done((bf16[8,272,128]{2,1,0:T(8,128)(2,1)}, bf16[8,272,128]{2,1,0:T(8,128)(2,1)S(1)}, u32[]{:S(2)}, u32[]{:S(2)}) %collective-permute-start.5) | collective-permute-done | bytes 557088 | tf_op jit(solution)/shard_map/ppermute | solution.py:313
  82.7 4.3 %join.1 = bf16[8,272,128]{2,1,0:T(8,128)(2,1)} custom-call(bf16[8,272,128]{2,1,0:T(8,128)(2,1)S(1)} %prompt.4.refs_0_, bf16[8,272,128]{2,1,0:T(8,128)(2,1)S(1)} %collective-permute-done.1.refs_1_, bf16[8,272,128]{2,1,0:T(8,128)(2,1)S(1)} %collective-permute-done.3.refs_2_, bf16[8,272,128]{2,1,0:T(8,128)(2,1)S(1)} %collective-permute-done.5.refs_3_), custom_call_target="tpu_custom_call" | custom-call | tf_op jit(solution)/shard_map/join/pallas_call | solution.py:379
  87.0 5.1 %all-to-all-start.1 = ((bf16[8,272,128]{2,1,0:T(8,128)(2,1)}), bf16[8,272,128]{2,1,0:T(8,128)(2,1)S(1)}, u32[]{:S(2)}, u32[]{:S(2)}) async-start(bf16[8,272,128]{2,1,0:T(8,128)(2,1)} %join.1), calls=%async_computation.1 | async-start | bytes 1114112 | tf_op jit(solution)/shard_map/all_to_all | solution.py:401
  92.1 0.0 copy-done.1
  92.1 0.1 collective-permute-start.6
  92.2 2.7 %collective-permute-start.7 = (bf16[1024,256]{1,0:T(8,128)(2,1)S(1)}, bf16[1024,256]{1,0:T(8,128)(2,1)}, u32[]{:S(2)}, u32[]{:S(2)}) collective-permute-start(bf16[1024,256]{1,0:T(8,128)(2,1)S(1)} %copy-done.1), channel_id=1, source_target_pairs={{0,192},{8,200},{16,208},{24,216},{32,224},{40,232},{48,240},{56,2... | collective-permute-start | bytes 1572872 | tf_op jit(solution)/shard_map/ppermute | solution.py:313
  94.9 0.1 min.16
  95.0 0.2 copy.14
  95.2 0.1 and.26
  95.3 0.0 copy-done.6
  95.4 0.0 copy-start
  95.4 0.0 copy-start.4
  95.4 7.5 %gather_fusion = bf16[1024,256]{1,0:T(8,128)(2,1)} fusion(bf16[8192,256]{1,0:T(8,128)(2,1)} %param.18, s32[1024]{0:T(1024)S(1)} %broadcast_clamp_fusion), kind=kCustom, calls=%fused_computation | custom fusion | bytes 1052672 | tf_op jit(solution)/shard_map/jit(_take)/gather | solution.py:405
  102.8 0.0 copy-start.5
  102.9 0.0 copy-done
  102.9 0.0 copy-done.4
  102.9 2.7 %own.1 = (f32[256,128]{1,0:T(8,128)S(1)}, f32[256,128]{1,0:T(8,128)S(1)}, f32[256,128]{1,0:T(8,128)S(1)}) custom-call(s32[8]{0:T(128)S(1)} %copy-done.4, bf16[256,128]{1,0:T(8,128)(2,1)S(1)} %bitcast.22, bf16[2,8,512,128]{3,2,1,0:T(8,128)(2,1)S(1)} %bitcast.19, bf16[2,8,16,128]{3,2,1,0:T(8,128)(2,1)S(1)} %pad.9.fresh_ref), custom_call_target="tpu_custom_call" | custom-call | tf_op jit(solution)/shard_map/own/pallas_call | solution.py:390
  105.6 0.0 copy-start.2
  105.7 0.0 copy-done.5
  105.7 0.3 select_select_fusion
  106.0 0.0 collective-permute-done.6.refs_2_
  106.0 0.3 copy-done.2
  106.3 0.0 collective-permute-done.7.refs_4_
  106.3 0.2 all-to-all-done.1.parts_ref
  106.5 0.0 copy-start.3
  106.5 0.9 copy-done.3
  107.4 0.7 merge.1
  108.2 0.9 broadcast_in_dim.39
  109.0 6.4 %all-to-all-start.2 = ((bf16[8,32,1024]{2,1,0:T(8,128)(2,1)}), bf16[8,32,1024]{2,1,0:T(8,128)(2,1)S(1)}, u32[]{:S(2)}, u32[]{:S(2)}) async-start(bf16[8,32,1024]{2,1,0:T(8,128)(2,1)} %broadcast_in_dim.39), calls=%async_computation.2 | async-start | bytes 1048576 | tf_op jit(solution)/shard_map/all_to_all | solution.py:304
  115.4 0.0 collective-permute-start.8
  115.5 9.8 %collective-permute-done.8.refs_3_ = bf16[1024,256]{1,0:T(8,128)(2,1)S(1)} collective-permute-done((bf16[1024,256]{1,0:T(8,128)(2,1)S(1)}, bf16[1024,256]{1,0:T(8,128)(2,1)S(1)}, u32[]{:S(2)}, u32[]{:S(2)}) %collective-permute-start.8) | collective-permute-done | bytes 524320 | tf_op jit(solution)/shard_map/ppermute | solution.py:313
  125.3 2.2 %all-to-all-done.2 = bf16[8,32,1024]{2,1,0:T(8,128)(2,1)S(1)} async-done(((bf16[8,32,1024]{2,1,0:T(8,128)(2,1)}), bf16[8,32,1024]{2,1,0:T(8,128)(2,1)S(1)}, u32[]{:S(2)}, u32[]{:S(2)}) %all-to-all-start.2) | async-done | bytes 524320 | tf_op jit(solution)/shard_map/all_to_all | solution.py:304
  127.5 1.9 %project.1 = bf16[4,256,256]{2,1,0:T(8,128)(2,1)S(1)} custom-call(s32[1]{0:T(128)} %bitcast.chip_ref, bf16[256,1024]{1,0:T(8,128)(2,1)S(1)} %bitcast.20, bf16[1024,256]{1,0:T(8,128)(2,1)S(1)} %copy-done.1, bf16[1024,256]{1,0:T(8,128)(2,1)} %collective-permute-done.6.refs_2_, bf16[1024,256]{1,0:T(8,128)(2,1)S(1)} %collective-permute-done.8.refs_3_, ...), custom_call_target="tpu_custom_call" | custom-call | tf_op jit(solution)/shard_map/project/pallas_call | solution.py:423
  129.4 9.3 %all_to_all.26 = bf16[4,256,256]{2,1,0:T(8,128)(2,1)S(1)} all-to-all(bf16[4,256,256]{2,1,0:T(8,128)(2,1)S(1)} %project.1), channel_id=1, replica_groups={{0,64,128,192},{8,72,136,200},{16,80,144,208},{24,88,152,216},{32,96,16..., dimensions={0} | all-to-all | bytes 1048576 | tf_op jit(solution)/shard_map/all_to_all | solution.py:433
  138.8 0.2 fusion
  138.9 21.2 %all_to_all.27 = bf16[8,128,256]{2,1,0:T(8,128)(2,1)S(1)} all-to-all(bf16[8,128,256]{2,1,0:T(8,128)(2,1)S(1)} %bitcast.23), channel_id=1, replica_groups=mesh['seq'=32,'head'=8] {'head'}, dimensions={0} | all-to-all | bytes 1048576 | tf_op jit(solution)/shard_map/all_to_all | solution.py:436
  160.1 0.1 reduce_sum.12
  160.2 0.7 reshape.100
  (9 shorter events, 0.1 us)
Async XLA Ops:
  26.9 12.6 %collective-permute-start = (bf16[8,272,128]{2,1,0:T(8,128)(2,1)S(1)}, bf16[8,272,128]{2,1,0:T(8,128)(2,1)S(1)}, u32[]{:S(2)}, u32[]{:S(2)}) collective-permute-start(bf16[8,272,128]{2,1,0:T(8,128)(2,1)S(1)} %all_to_all.25.q_ref), channel_id=1, source_target_pairs={{0,64},{8,72},{16,80},{24,88},{32,96},{40,104},{48,112},{56,120},{... | collective-permute-start | bytes 1671176 | tf_op jit(solution)/shard_map/ppermute | solution.py:313
  28.1 21.4 %collective-permute-start.2 = (bf16[8,272,128]{2,1,0:T(8,128)(2,1)S(1)}, bf16[8,272,128]{2,1,0:T(8,128)(2,1)S(1)}, u32[]{:S(2)}, u32[]{:S(2)}) collective-permute-start(bf16[8,272,128]{2,1,0:T(8,128)(2,1)S(1)} %all_to_all.25.q_ref), channel_id=1, source_target_pairs={{0,192},{8,200},{16,208},{24,216},{32,224},{40,232},{48,240},{56,2... | collective-permute-start | bytes 1671176 | tf_op jit(solution)/shard_map/ppermute | solution.py:313
  29.6 28.8 %collective-permute-start.4 = (bf16[8,272,128]{2,1,0:T(8,128)(2,1)S(1)}, bf16[8,272,128]{2,1,0:T(8,128)(2,1)S(1)}, u32[]{:S(2)}, u32[]{:S(2)}) collective-permute-start(bf16[8,272,128]{2,1,0:T(8,128)(2,1)S(1)} %all_to_all.25.q_ref), channel_id=1, source_target_pairs={{0,128},{8,136},{16,144},{24,152},{32,160},{40,168},{48,176},{56,1... | collective-permute-start | bytes 1671176 | tf_op jit(solution)/shard_map/ppermute | solution.py:313
  48.1 21.0 %collective-permute-start.1 = (bf16[8,272,128]{2,1,0:T(8,128)(2,1)}, bf16[8,272,128]{2,1,0:T(8,128)(2,1)S(1)}, u32[]{:S(2)}, u32[]{:S(2)}) collective-permute-start(bf16[8,272,128]{2,1,0:T(8,128)(2,1)} %prompt.5), channel_id=1, source_target_pairs={{0,192},{8,200},{16,208},{24,216},{32,224},{40,232},{48,240},{56,2... | collective-permute-start | bytes 1671176 | tf_op jit(solution)/shard_map/ppermute | solution.py:313
  58.1 10.7 %copy-start.7 = (s32[256,4]{0,1:T(4,128)S(1)}, s32[256,4]{0,1:T(4,128)}, u32[]{:S(2)}) copy-start(s32[256,4]{0,1:T(4,128)} %param.17) | copy-start | bytes 12292
  58.1 11.0 %collective-permute-start.3 = (bf16[8,272,128]{2,1,0:T(8,128)(2,1)}, bf16[8,272,128]{2,1,0:T(8,128)(2,1)S(1)}, u32[]{:S(2)}, u32[]{:S(2)}) collective-permute-start(bf16[8,272,128]{2,1,0:T(8,128)(2,1)} %prompt.6), channel_id=1, source_target_pairs={{0,64},{8,72},{16,80},{24,88},{32,96},{40,104},{48,112},{56,120},{... | collective-permute-start | bytes 1671176 | tf_op jit(solution)/shard_map/ppermute | solution.py:313
  67.0 15.7 %collective-permute-start.5 = (bf16[8,272,128]{2,1,0:T(8,128)(2,1)}, bf16[8,272,128]{2,1,0:T(8,128)(2,1)S(1)}, u32[]{:S(2)}, u32[]{:S(2)}) collective-permute-start(bf16[8,272,128]{2,1,0:T(8,128)(2,1)} %prompt.7), channel_id=1, source_target_pairs={{0,128},{8,136},{16,144},{24,152},{32,160},{40,168},{48,176},{56,1... | collective-permute-start | bytes 1671176 | tf_op jit(solution)/shard_map/ppermute | solution.py:313
  68.8 23.3 %copy-start.1 = (bf16[1024,256]{1,0:T(8,128)(2,1)S(1)}, bf16[1024,256]{1,0:T(8,128)(2,1)}, u32[]{:S(2)}) copy-start(bf16[1024,256]{1,0:T(8,128)(2,1)} %refs_1_) | copy-start | bytes 1572868
  69.0 26.4 %copy-start.6 = (bf16[2,4,8,1,128]{4,2,3,1,0:T(8,128)(2,1)S(1)}, bf16[2,4,8,1,128]{4,2,3,1,0:T(8,128)(2,1)}, u32[]{:S(2)}) copy-start(bf16[2,4,8,1,128]{4,2,3,1,0:T(8,128)(2,1)} %param.11) | copy-start | bytes 49156
  87.0 19.5 %all-to-all-start.1 = ((bf16[8,272,128]{2,1,0:T(8,128)(2,1)}), bf16[8,272,128]{2,1,0:T(8,128)(2,1)S(1)}, u32[]{:S(2)}, u32[]{:S(2)}) async-start(bf16[8,272,128]{2,1,0:T(8,128)(2,1)} %join.1), calls=%async_computation.1 | async-start | bytes 1114112 | tf_op jit(solution)/shard_map/all_to_all | solution.py:401
  92.1 13.9 %collective-permute-start.6 = (bf16[1024,256]{1,0:T(8,128)(2,1)S(1)}, bf16[1024,256]{1,0:T(8,128)(2,1)}, u32[]{:S(2)}, u32[]{:S(2)}) collective-permute-start(bf16[1024,256]{1,0:T(8,128)(2,1)S(1)} %copy-done.1), channel_id=1, source_target_pairs={{0,64},{8,72},{16,80},{24,88},{32,96},{40,104},{48,112},{56,120},{... | collective-permute-start | bytes 1572872 | tf_op jit(solution)/shard_map/ppermute | solution.py:313
  92.2 14.1 %collective-permute-start.7 = (bf16[1024,256]{1,0:T(8,128)(2,1)S(1)}, bf16[1024,256]{1,0:T(8,128)(2,1)}, u32[]{:S(2)}, u32[]{:S(2)}) collective-permute-start(bf16[1024,256]{1,0:T(8,128)(2,1)S(1)} %copy-done.1), channel_id=1, source_target_pairs={{0,192},{8,200},{16,208},{24,216},{32,224},{40,232},{48,240},{56,2... | collective-permute-start | bytes 1572872 | tf_op jit(solution)/shard_map/ppermute | solution.py:313
  95.4 7.5 %copy-start = (bf16[2,8,512,1,128]{4,2,3,1,0:T(8,128)(2,1)S(1)}, bf16[2,8,512,1,128]{4,2,3,1,0:T(8,128)(2,1)}, u32[]{:S(2)}) copy-start(bf16[2,8,512,1,128]{4,2,3,1,0:T(8,128)(2,1)} %param.14) | copy-start | bytes 6291460
  95.4 7.5 %copy-start.4 = (s32[8]{0:T(128)S(1)}, s32[8]{0:T(128)}, u32[]{:S(2)}) copy-start(s32[8]{0:T(128)} %len_ref.1) | copy-start | bytes 100
  102.8 2.8 %copy-start.5 = (bf16[1024,256]{1,0:T(8,128)(2,1)S(1)}, bf16[1024,256]{1,0:T(8,128)(2,1)}, u32[]{:S(2)}) copy-start(bf16[1024,256]{1,0:T(8,128)(2,1)} %gather_fusion) | copy-start | bytes 1572868
  105.6 0.7 copy-start.2
  106.5 0.9 copy-start.3
  109.0 18.5 %all-to-all-start.2 = ((bf16[8,32,1024]{2,1,0:T(8,128)(2,1)}), bf16[8,32,1024]{2,1,0:T(8,128)(2,1)S(1)}, u32[]{:S(2)}, u32[]{:S(2)}) async-start(bf16[8,32,1024]{2,1,0:T(8,128)(2,1)} %broadcast_in_dim.39), calls=%async_computation.2 | async-start | bytes 1048576 | tf_op jit(solution)/shard_map/all_to_all | solution.py:304
  115.4 9.9 %collective-permute-start.8 = (bf16[1024,256]{1,0:T(8,128)(2,1)S(1)}, bf16[1024,256]{1,0:T(8,128)(2,1)S(1)}, u32[]{:S(2)}, u32[]{:S(2)}) collective-permute-start(bf16[1024,256]{1,0:T(8,128)(2,1)S(1)} %copy-done.1), channel_id=1, source_target_pairs={{0,128},{8,136},{16,144},{24,152},{32,160},{40,168},{48,176},{56,1... | collective-permute-start | bytes 1572872 | tf_op jit(solution)/shard_map/ppermute | solution.py:313

commit v3 on v2

--- a/solution.py
+++ b/solution.py
@@ -94,7 +94,7 @@
     def load(p):
         return (
             pltpu.make_async_copy(k_hbm.at[p], k_ref.at[p], k_sem.at[p]),
-            pltpu.make_async_copy(v_hbm.at[p], v_ref.at[p], v_sem.at[p]),
+            pltpu.make_async_copy(v_hbm.at[p], v_ref.at[p, :, :128], v_sem.at[p]),
         )
 
     def finish(p, carry):
@@ -108,6 +108,8 @@
     for p in range(prompts):
         for copy in load(p):
             copy.start()
+    for p in range(prompts):
+        v_ref[p, :, 128:] = jnp.ones((v_ref.shape[1], 128), jnp.bfloat16)
     ids_copy.wait()
     blocks = slot_table(owners * OWNER_ROWS, prompts, ids_ref, slot_ref, next_ref)
 
@@ -123,20 +125,20 @@
     def score(b, at):
         _, where, prompt = locate(b)
         q = jnp.concatenate([q_ref[o, w, :] for o, w in where], axis=0)
-        score_ref[at] = lax.dot_general(
+        score_ref[at] = scale * lax.dot_general(
             q, k_ref[prompt], (((1,), (1,)), ((), ())), preferred_element_type=jnp.float32
         )
 
     def mix(b, at):
         rows, where, prompt = locate(b)
         s = score_ref[at]
-        top = jnp.max(s, axis=-1, keepdims=True) * scale
-        p = jnp.exp2(s * scale - top)
-        total = jnp.sum(p, axis=-1, keepdims=True)
+        top = jnp.max(s, axis=-1, keepdims=True)
+        p = jnp.exp2(s - top)
         mixed = jnp.dot(
             p.astype(jnp.bfloat16), v_ref[prompt], preferred_element_type=jnp.float32
         )
-        mixed = (mixed / total).astype(jnp.bfloat16)
+        total = mixed[:, 128:]
+        mixed = (mixed[:, :128] / total).astype(jnp.bfloat16)
         hi, mid, lo = three_terms(top)
         lane = lax.broadcasted_iota(jnp.int32, (queries, 128), 1)
         at_row = lax.broadcasted_iota(jnp.int32, (queries, 128), 0) % per_row
@@ -205,20 +207,31 @@
     n = len(parts)
     body_rows = OWNER_ROWS * per_row
     lane = lax.broadcasted_iota(jnp.int32, (OWNER_ROWS, 128), 1) // per_row
+    query = lax.broadcasted_iota(jnp.int32, (per_row, 128), 1) % per_row
+    diagonal = query == lax.broadcasted_iota(jnp.int32, (per_row, 128), 0)
     for o in range(out_ref.shape[0]):
         stats = [read_stats(per_row, ref[o : o + 1, body_rows : body_rows + PACK, :]) for ref in parts]
         tops = [t[0] for t, _ in stats]
         peak = functools.reduce(jnp.maximum, tops)
         weights = [total[0] * jnp.exp2(t - peak) for t, (_, total) in zip(tops, stats)]
         summed = functools.reduce(jnp.add, weights)
-        table = jnp.concatenate([w / summed for w in weights], axis=0)
-        table = jnp.transpose(table)[:per_row, :]
+        share = weights[-1] / summed
+        for i in reversed(range(n)):
+            placed = pltpu.roll(weights[i] / summed, i * per_row, 1) if i else weights[i] / summed
+            share = jnp.where(lane == i, placed, share)
+        high = share.astype(jnp.bfloat16).astype(jnp.float32)
+        low = share - high
         for j in range(OWNER_ROWS):
             span = slice(j * per_row, (j + 1) * per_row)
+            stacked = jnp.concatenate([part[o, span, :] for part in parts], axis=0)
             acc = jnp.zeros((per_row, 128), jnp.float32)
-            for i in range(n):
-                at = i * OWNER_ROWS + j
-                acc += table[:, at : at + 1] * parts[i][o, span, :].astype(jnp.float32)
+            for piece in (high, low):
+                rows = jnp.broadcast_to(piece[j : j + 1, :], (per_row, 128))
+                acc += jnp.dot(
+                    jnp.where(diagonal, rows, 0.0).astype(jnp.bfloat16),
+                    stacked,
+                    preferred_element_type=jnp.float32,
+                )
             out_ref[o, span, :] = acc.astype(jnp.bfloat16)
         hi, mid, lo = three_terms(peak)
         stat = jnp.where(
@@ -350,7 +363,7 @@
         out_specs=VMEM,
         scratch_shapes=[
             pltpu.VMEM(keys.shape, jnp.bfloat16),
-            pltpu.VMEM(values.shape, jnp.bfloat16),
+            pltpu.VMEM((prompts, positions, 2 * head_dim), jnp.bfloat16),
             pltpu.VMEM((chunk_rows, 128), jnp.float32),
             pltpu.VMEM((2 * DEPTH, BLOCK_ROWS * per_row, positions), jnp.float32),
             pltpu.SMEM((blocks * BLOCK_ROWS,), jnp.int32),

time: 162 us -> 158 us (0.975)
  Pallas kernels: 43.2 us -> 38.3 us
  waiting for transfers between devices: 26.5 us -> 28.4 us
    pallas_call x4, Pallas kernels: 33.5 us -> 30.8 us  [partial_of(): return attend(q, keys, values)]
    pallas_call x1, Pallas kernels: 4.33 us -> 2.18 us  [shards(): pl.pallas_call(functools.partial(join_kernel, per_row), out_shape=payload...]
    ppermute x9, waiting for transfers between devices: 24.1 us -> 26 us  [shift_x(): return lax.ppermute(x, 'seq', pairs)]
  transfers between devices with their start and end apart: 11 -> 11, of which waited for: 5 -> 5; matrix products, arithmetic and copies ran while one was open for 5% -> 5% of each run, Pallas kernels for 23% -> 21%
where the time goes in v3:
time: 158 us; the launch traced here: 157 us
  blocking collectives  55.9 us (35%)
  Pallas kernels  38.3 us (24%)
  waiting for transfers between devices  28.4 us (18%)
  starting transfers between devices  21.4 us (14%)
  local copies, waits for them, and re-layouts  11.8 us (7%)
    pallas_call x4, Pallas kernels, partial_of(): return attend(q, keys, values)  30.8 us
    ppermute x9, waiting for transfers between devices, shift_x(): return lax.ppermute(x, 'seq', pairs)  26 us
    all_to_all x1, blocking collectives, spread(): lax.all_to_all(jnp.broadcast_to(x[None], (n,) + x.shape), 'seq', 0, 0, ax...  25.3 us
    all_to_all x1, blocking collectives, shards(): lax.all_to_all(terms.reshape(heads, -1, terms.shape[1]), 'head', 0, 0)  21.2 us
    ppermute x9, starting transfers between devices, shift_x(): return lax.ppermute(x, 'seq', pairs)  10.2 us
    all_to_all x1, blocking collectives, shards(): lax.all_to_all(projected, 'seq', 0, 0, axis_index_groups=X_GROUPS)  9.33 us
    gather x1, local copies, waits for them, and re-layouts, shards(): jnp.take(embedding, jnp.clip(local_ids, 0, vocab_own - 1), axis=0)  7.46 us
    all_to_all x1, starting transfers between devices, spread(): lax.all_to_all(jnp.broadcast_to(x[None], (n,) + x.shape), 'seq', 0, 0, ax...  6.34 us
  transfers between devices with their start and end apart: 11, of which 5 were waited for; matrix products, arithmetic and copies ran while one was open for 5% of the time, Pallas kernels for 21%

profile of v3, /device:TPU:1, one launch (start us, length us, event | category | flops | bytes accessed | tf_op | source)
XLA Modules:
  0.0 157.4 jit_solution(10109082421594771998)
XLA Ops:
  0.0 0.7 convert_bitcast_fusion
  0.7 0.9 copy.13
  1.5 0.1 broadcast_in_dim.34
  1.6 25.3 %all_to_all.25.q_ref = bf16[8,272,128]{2,1,0:T(8,128)(2,1)S(1)} all-to-all(bf16[8,272,128]{2,1,0:T(8,128)(2,1)S(1)} %broadcast_in_dim.34), channel_id=1, replica_groups={{0,8,16,24,32,40,48,56},{64,72,80,88,96,104,112,120},{128,136,144,152,1..., dimensions={0} | all-to-all | bytes 1114112 | tf_op jit(solution)/shard_map/all_to_all | solution.py:317
  26.9 1.2 collective-permute-start
  28.1 1.5 collective-permute-start.2
  29.6 1.5 collective-permute-start.4
  31.1 7.0 %prompt.4.refs_0_ = bf16[8,272,128]{2,1,0:T(8,128)(2,1)S(1)} custom-call(bf16[8,272,128]{2,1,0:T(8,128)(2,1)S(1)} %all_to_all.25.q_ref, bf16[8,1024,128]{2,1,0:T(8,128)(2,1)} %bitcast.27, bf16[8,1024,128]{2,1,0:T(8,128)(2,1)} %bitcast.31), custom_call_target="tpu_custom_call" | custom-call | flops 2147483648 | bytes 4194304 | tf_op jit(solution)/shard_map/prompt/pallas_call | solution.py:385
  38.1 1.4 collective-permute-done.q_ref
  39.5 7.9 %prompt.5 = bf16[8,272,128]{2,1,0:T(8,128)(2,1)} custom-call(bf16[8,272,128]{2,1,0:T(8,128)(2,1)S(1)} %collective-permute-done.q_ref, bf16[8,1024,128]{2,1,0:T(8,128)(2,1)} %bitcast.28, bf16[8,1024,128]{2,1,0:T(8,128)(2,1)} %bitcast.32), custom_call_target="tpu_custom_call" | custom-call | flops 2147483648 | bytes 4194304 | tf_op jit(solution)/shard_map/prompt/pallas_call | solution.py:385
  47.4 1.4 collective-permute-start.1
  48.8 0.0 collective-permute-done.2.q_ref
  48.8 7.9 %prompt.6 = bf16[8,272,128]{2,1,0:T(8,128)(2,1)} custom-call(bf16[8,272,128]{2,1,0:T(8,128)(2,1)S(1)} %collective-permute-done.2.q_ref, bf16[8,1024,128]{2,1,0:T(8,128)(2,1)} %bitcast.29, bf16[8,1024,128]{2,1,0:T(8,128)(2,1)} %bitcast.33), custom_call_target="tpu_custom_call" | custom-call | flops 2147483648 | bytes 4194304 | tf_op jit(solution)/shard_map/prompt/pallas_call | solution.py:385
  56.6 0.0 copy-start.7
  56.7 0.3 collective-permute-start.3
  56.9 0.0 collective-permute-done.4.q_ref
  56.9 8.1 %prompt.7 = bf16[8,272,128]{2,1,0:T(8,128)(2,1)} custom-call(bf16[8,272,128]{2,1,0:T(8,128)(2,1)S(1)} %collective-permute-done.4.q_ref, bf16[8,1024,128]{2,1,0:T(8,128)(2,1)} %bitcast.30, bf16[8,1024,128]{2,1,0:T(8,128)(2,1)} %bitcast.34), custom_call_target="tpu_custom_call" | custom-call | flops 2147483648 | bytes 4194304 | tf_op jit(solution)/shard_map/prompt/pallas_call | solution.py:385
  65.0 1.6 %collective-permute-start.5 = (bf16[8,272,128]{2,1,0:T(8,128)(2,1)}, bf16[8,272,128]{2,1,0:T(8,128)(2,1)S(1)}, u32[]{:S(2)}, u32[]{:S(2)}) collective-permute-start(bf16[8,272,128]{2,1,0:T(8,128)(2,1)} %prompt.7), channel_id=1, source_target_pairs={{0,128},{8,136},{16,144},{24,152},{32,160},{40,168},{48,176},{56,1... | collective-permute-start | bytes 1671176 | tf_op jit(solution)/shard_map/ppermute | solution.py:326
  66.6 0.0 copy-done.7
  66.6 0.0 copy-start.1
  66.6 0.1 copy.15
  66.8 0.0 copy-start.6
  66.8 0.1 min.18
  66.9 0.0 collective-permute-done.1.refs_1_
  66.9 0.0 collective-permute-done.3.refs_2_
  66.9 14.6 %collective-permute-done.5.refs_3_ = bf16[8,272,128]{2,1,0:T(8,128)(2,1)S(1)} collective-permute-done((bf16[8,272,128]{2,1,0:T(8,128)(2,1)}, bf16[8,272,128]{2,1,0:T(8,128)(2,1)S(1)}, u32[]{:S(2)}, u32[]{:S(2)}) %collective-permute-start.5) | collective-permute-done | bytes 557088 | tf_op jit(solution)/shard_map/ppermute | solution.py:326
  81.5 2.2 %join.1 = bf16[8,272,128]{2,1,0:T(8,128)(2,1)} custom-call(bf16[8,272,128]{2,1,0:T(8,128)(2,1)S(1)} %prompt.4.refs_0_, bf16[8,272,128]{2,1,0:T(8,128)(2,1)S(1)} %collective-permute-done.1.refs_1_, bf16[8,272,128]{2,1,0:T(8,128)(2,1)S(1)} %collective-permute-done.3.refs_2_, bf16[8,272,128]{2,1,0:T(8,128)(2,1)S(1)} %collective-permute-done.5.refs_3_), custom_call_target="tpu_custom_call" | custom-call | tf_op jit(solution)/shard_map/join/pallas_call | solution.py:392
  83.7 4.9 %all-to-all-start.1 = ((bf16[8,272,128]{2,1,0:T(8,128)(2,1)}), bf16[8,272,128]{2,1,0:T(8,128)(2,1)S(1)}, u32[]{:S(2)}, u32[]{:S(2)}) async-start(bf16[8,272,128]{2,1,0:T(8,128)(2,1)} %join.1), calls=%async_computation.1 | async-start | bytes 1114112 | tf_op jit(solution)/shard_map/all_to_all | solution.py:414
  88.6 0.0 copy-done.1
  88.6 0.1 collective-permute-start.6
  88.7 2.7 %collective-permute-start.7 = (bf16[1024,256]{1,0:T(8,128)(2,1)S(1)}, bf16[1024,256]{1,0:T(8,128)(2,1)}, u32[]{:S(2)}, u32[]{:S(2)}) collective-permute-start(bf16[1024,256]{1,0:T(8,128)(2,1)S(1)} %copy-done.1), channel_id=1, source_target_pairs={{0,192},{8,200},{16,208},{24,216},{32,224},{40,232},{48,240},{56,2... | collective-permute-start | bytes 1572872 | tf_op jit(solution)/shard_map/ppermute | solution.py:326
  91.4 0.1 min.16
  91.5 0.2 copy.14
  91.7 0.1 and.26
  91.8 0.0 copy-done.6
  91.8 0.0 copy-start
  91.8 0.0 copy-start.4
  91.9 7.5 %gather_fusion = bf16[1024,256]{1,0:T(8,128)(2,1)} fusion(bf16[8192,256]{1,0:T(8,128)(2,1)} %param.18, s32[1024]{0:T(1024)S(1)} %broadcast_clamp_fusion), kind=kCustom, calls=%fused_computation | custom fusion | bytes 1052672 | tf_op jit(solution)/shard_map/jit(_take)/gather | solution.py:418
  99.3 0.0 copy-start.5
  99.3 0.0 copy-done
  99.3 0.0 copy-done.4
  99.4 2.7 %own.1 = (f32[256,128]{1,0:T(8,128)S(1)}, f32[256,128]{1,0:T(8,128)S(1)}, f32[256,128]{1,0:T(8,128)S(1)}) custom-call(s32[8]{0:T(128)S(1)} %copy-done.4, bf16[256,128]{1,0:T(8,128)(2,1)S(1)} %bitcast.22, bf16[2,8,512,128]{3,2,1,0:T(8,128)(2,1)S(1)} %bitcast.19, bf16[2,8,16,128]{3,2,1,0:T(8,128)(2,1)S(1)} %pad.9.fresh_ref), custom_call_target="tpu_custom_call" | custom-call | tf_op jit(solution)/shard_map/own/pallas_call | solution.py:403
  102.1 0.0 copy-start.2
  102.1 0.0 copy-done.5
  102.1 0.3 select_select_fusion
  102.5 0.0 collective-permute-done.6.refs_2_
  102.5 0.3 copy-done.2
  102.8 0.0 collective-permute-done.7.refs_4_
  102.8 0.3 all-to-all-done.1.parts_ref
  103.1 0.0 copy-start.3
  103.1 0.9 copy-done.3
  104.0 0.7 merge.1
  104.7 0.9 broadcast_in_dim.39
  105.6 6.3 %all-to-all-start.2 = ((bf16[8,32,1024]{2,1,0:T(8,128)(2,1)}), bf16[8,32,1024]{2,1,0:T(8,128)(2,1)S(1)}, u32[]{:S(2)}, u32[]{:S(2)}) async-start(bf16[8,32,1024]{2,1,0:T(8,128)(2,1)} %broadcast_in_dim.39), calls=%async_computation.2 | async-start | bytes 1048576 | tf_op jit(solution)/shard_map/all_to_all | solution.py:317
  111.9 0.0 collective-permute-start.8
  111.9 9.9 %collective-permute-done.8.refs_3_ = bf16[1024,256]{1,0:T(8,128)(2,1)S(1)} collective-permute-done((bf16[1024,256]{1,0:T(8,128)(2,1)S(1)}, bf16[1024,256]{1,0:T(8,128)(2,1)S(1)}, u32[]{:S(2)}, u32[]{:S(2)}) %collective-permute-start.8) | collective-permute-done | bytes 524320 | tf_op jit(solution)/shard_map/ppermute | solution.py:326
  121.8 2.2 %all-to-all-done.2 = bf16[8,32,1024]{2,1,0:T(8,128)(2,1)S(1)} async-done(((bf16[8,32,1024]{2,1,0:T(8,128)(2,1)}), bf16[8,32,1024]{2,1,0:T(8,128)(2,1)S(1)}, u32[]{:S(2)}, u32[]{:S(2)}) %all-to-all-start.2) | async-done | bytes 524320 | tf_op jit(solution)/shard_map/all_to_all | solution.py:317
  124.0 1.9 %project.1 = bf16[4,256,256]{2,1,0:T(8,128)(2,1)S(1)} custom-call(s32[1]{0:T(128)} %bitcast.chip_ref, bf16[256,1024]{1,0:T(8,128)(2,1)S(1)} %bitcast.20, bf16[1024,256]{1,0:T(8,128)(2,1)S(1)} %copy-done.1, bf16[1024,256]{1,0:T(8,128)(2,1)} %collective-permute-done.6.refs_2_, bf16[1024,256]{1,0:T(8,128)(2,1)S(1)} %collective-permute-done.8.refs_3_, ...), custom_call_target="tpu_custom_call" | custom-call | tf_op jit(solution)/shard_map/project/pallas_call | solution.py:436
  125.9 9.3 %all_to_all.26 = bf16[4,256,256]{2,1,0:T(8,128)(2,1)S(1)} all-to-all(bf16[4,256,256]{2,1,0:T(8,128)(2,1)S(1)} %project.1), channel_id=1, replica_groups={{0,64,128,192},{8,72,136,200},{16,80,144,208},{24,88,152,216},{32,96,16..., dimensions={0} | all-to-all | bytes 1048576 | tf_op jit(solution)/shard_map/all_to_all | solution.py:446
  135.2 0.2 fusion
  135.4 21.2 %all_to_all.27 = bf16[8,128,256]{2,1,0:T(8,128)(2,1)S(1)} all-to-all(bf16[8,128,256]{2,1,0:T(8,128)(2,1)S(1)} %bitcast.23), channel_id=1, replica_groups=mesh['seq'=32,'head'=8] {'head'}, dimensions={0} | all-to-all | bytes 1048576 | tf_op jit(solution)/shard_map/all_to_all | solution.py:449
  156.6 0.1 reduce_sum.12
  156.7 0.7 reshape.100
  (9 shorter events, 0.1 us)
Async XLA Ops:
  26.9 12.6 %collective-permute-start = (bf16[8,272,128]{2,1,0:T(8,128)(2,1)S(1)}, bf16[8,272,128]{2,1,0:T(8,128)(2,1)S(1)}, u32[]{:S(2)}, u32[]{:S(2)}) collective-permute-start(bf16[8,272,128]{2,1,0:T(8,128)(2,1)S(1)} %all_to_all.25.q_ref), channel_id=1, source_target_pairs={{0,64},{8,72},{16,80},{24,88},{32,96},{40,104},{48,112},{56,120},{... | collective-permute-start | bytes 1671176 | tf_op jit(solution)/shard_map/ppermute | solution.py:326
  28.1 20.7 %collective-permute-start.2 = (bf16[8,272,128]{2,1,0:T(8,128)(2,1)S(1)}, bf16[8,272,128]{2,1,0:T(8,128)(2,1)S(1)}, u32[]{:S(2)}, u32[]{:S(2)}) collective-permute-start(bf16[8,272,128]{2,1,0:T(8,128)(2,1)S(1)} %all_to_all.25.q_ref), channel_id=1, source_target_pairs={{0,192},{8,200},{16,208},{24,216},{32,224},{40,232},{48,240},{56,2... | collective-permute-start | bytes 1671176 | tf_op jit(solution)/shard_map/ppermute | solution.py:326
  29.6 27.3 %collective-permute-start.4 = (bf16[8,272,128]{2,1,0:T(8,128)(2,1)S(1)}, bf16[8,272,128]{2,1,0:T(8,128)(2,1)S(1)}, u32[]{:S(2)}, u32[]{:S(2)}) collective-permute-start(bf16[8,272,128]{2,1,0:T(8,128)(2,1)S(1)} %all_to_all.25.q_ref), channel_id=1, source_target_pairs={{0,128},{8,136},{16,144},{24,152},{32,160},{40,168},{48,176},{56,1... | collective-permute-start | bytes 1671176 | tf_op jit(solution)/shard_map/ppermute | solution.py:326
  47.4 19.5 %collective-permute-start.1 = (bf16[8,272,128]{2,1,0:T(8,128)(2,1)}, bf16[8,272,128]{2,1,0:T(8,128)(2,1)S(1)}, u32[]{:S(2)}, u32[]{:S(2)}) collective-permute-start(bf16[8,272,128]{2,1,0:T(8,128)(2,1)} %prompt.5), channel_id=1, source_target_pairs={{0,192},{8,200},{16,208},{24,216},{32,224},{40,232},{48,240},{56,2... | collective-permute-start | bytes 1671176 | tf_op jit(solution)/shard_map/ppermute | solution.py:326
  56.6 10.0 %copy-start.7 = (s32[256,4]{0,1:T(4,128)S(1)}, s32[256,4]{0,1:T(4,128)}, u32[]{:S(2)}) copy-start(s32[256,4]{0,1:T(4,128)} %param.17) | copy-start | bytes 12292
  56.7 10.2 %collective-permute-start.3 = (bf16[8,272,128]{2,1,0:T(8,128)(2,1)}, bf16[8,272,128]{2,1,0:T(8,128)(2,1)S(1)}, u32[]{:S(2)}, u32[]{:S(2)}) collective-permute-start(bf16[8,272,128]{2,1,0:T(8,128)(2,1)} %prompt.6), channel_id=1, source_target_pairs={{0,64},{8,72},{16,80},{24,88},{32,96},{40,104},{48,112},{56,120},{... | collective-permute-start | bytes 1671176 | tf_op jit(solution)/shard_map/ppermute | solution.py:326
  65.0 16.6 %collective-permute-start.5 = (bf16[8,272,128]{2,1,0:T(8,128)(2,1)}, bf16[8,272,128]{2,1,0:T(8,128)(2,1)S(1)}, u32[]{:S(2)}, u32[]{:S(2)}) collective-permute-start(bf16[8,272,128]{2,1,0:T(8,128)(2,1)} %prompt.7), channel_id=1, source_target_pairs={{0,128},{8,136},{16,144},{24,152},{32,160},{40,168},{48,176},{56,1... | collective-permute-start | bytes 1671176 | tf_op jit(solution)/shard_map/ppermute | solution.py:326
  66.6 22.0 %copy-start.1 = (bf16[1024,256]{1,0:T(8,128)(2,1)S(1)}, bf16[1024,256]{1,0:T(8,128)(2,1)}, u32[]{:S(2)}) copy-start(bf16[1024,256]{1,0:T(8,128)(2,1)} %refs_1_) | copy-start | bytes 1572868
  66.8 25.1 %copy-start.6 = (bf16[2,4,8,1,128]{4,2,3,1,0:T(8,128)(2,1)S(1)}, bf16[2,4,8,1,128]{4,2,3,1,0:T(8,128)(2,1)}, u32[]{:S(2)}) copy-start(bf16[2,4,8,1,128]{4,2,3,1,0:T(8,128)(2,1)} %param.11) | copy-start | bytes 49156
  83.7 19.4 %all-to-all-start.1 = ((bf16[8,272,128]{2,1,0:T(8,128)(2,1)}), bf16[8,272,128]{2,1,0:T(8,128)(2,1)S(1)}, u32[]{:S(2)}, u32[]{:S(2)}) async-start(bf16[8,272,128]{2,1,0:T(8,128)(2,1)} %join.1), calls=%async_computation.1 | async-start | bytes 1114112 | tf_op jit(solution)/shard_map/all_to_all | solution.py:414
  88.6 13.9 %collective-permute-start.6 = (bf16[1024,256]{1,0:T(8,128)(2,1)S(1)}, bf16[1024,256]{1,0:T(8,128)(2,1)}, u32[]{:S(2)}, u32[]{:S(2)}) collective-permute-start(bf16[1024,256]{1,0:T(8,128)(2,1)S(1)} %copy-done.1), channel_id=1, source_target_pairs={{0,64},{8,72},{16,80},{24,88},{32,96},{40,104},{48,112},{56,120},{... | collective-permute-start | bytes 1572872 | tf_op jit(solution)/shard_map/ppermute | solution.py:326
  88.7 14.1 %collective-permute-start.7 = (bf16[1024,256]{1,0:T(8,128)(2,1)S(1)}, bf16[1024,256]{1,0:T(8,128)(2,1)}, u32[]{:S(2)}, u32[]{:S(2)}) collective-permute-start(bf16[1024,256]{1,0:T(8,128)(2,1)S(1)} %copy-done.1), channel_id=1, source_target_pairs={{0,192},{8,200},{16,208},{24,216},{32,224},{40,232},{48,240},{56,2... | collective-permute-start | bytes 1572872 | tf_op jit(solution)/shard_map/ppermute | solution.py:326
  91.8 7.5 %copy-start = (bf16[2,8,512,1,128]{4,2,3,1,0:T(8,128)(2,1)S(1)}, bf16[2,8,512,1,128]{4,2,3,1,0:T(8,128)(2,1)}, u32[]{:S(2)}) copy-start(bf16[2,8,512,1,128]{4,2,3,1,0:T(8,128)(2,1)} %param.14) | copy-start | bytes 6291460
  91.8 7.5 %copy-start.4 = (s32[8]{0:T(128)S(1)}, s32[8]{0:T(128)}, u32[]{:S(2)}) copy-start(s32[8]{0:T(128)} %len_ref.1) | copy-start | bytes 100
  99.3 2.8 %copy-start.5 = (bf16[1024,256]{1,0:T(8,128)(2,1)S(1)}, bf16[1024,256]{1,0:T(8,128)(2,1)}, u32[]{:S(2)}) copy-start(bf16[1024,256]{1,0:T(8,128)(2,1)} %gather_fusion) | copy-start | bytes 1572868
  102.1 0.7 copy-start.2
  103.1 0.9 copy-start.3
  105.6 18.4 %all-to-all-start.2 = ((bf16[8,32,1024]{2,1,0:T(8,128)(2,1)}), bf16[8,32,1024]{2,1,0:T(8,128)(2,1)S(1)}, u32[]{:S(2)}, u32[]{:S(2)}) async-start(bf16[8,32,1024]{2,1,0:T(8,128)(2,1)} %broadcast_in_dim.39), calls=%async_computation.2 | async-start | bytes 1048576 | tf_op jit(solution)/shard_map/all_to_all | solution.py:317
  111.9 9.9 %collective-permute-start.8 = (bf16[1024,256]{1,0:T(8,128)(2,1)S(1)}, bf16[1024,256]{1,0:T(8,128)(2,1)S(1)}, u32[]{:S(2)}, u32[]{:S(2)}) collective-permute-start(bf16[1024,256]{1,0:T(8,128)(2,1)S(1)} %copy-done.1), channel_id=1, source_target_pairs={{0,128},{8,136},{16,144},{24,152},{32,160},{40,168},{48,176},{56,1... | collective-permute-start | bytes 1572872 | tf_op jit(solution)/shard_map/ppermute | solution.py:326
